TPU v7x, 32 devices: a whole 2x2x4 slice. The times are simulated.
32 devices in a mesh: section: 4 (over y, x), rows: 8 (over z, core).
Axes of the slice: x: 2, y: 2, z: 4, core: 2. Of those that a mesh axis runs over, the one named last changes fastest.
Arguments:
- tokens: bfloat16 [8, 2048, 768], P(None, 'rows'), may hold values from -6 to 6
- cotangent: bfloat16 [8, 2048, 768], P(None, 'rows'), may hold values from -6 to 6
- segment_ids: int32 [8, 2048], replicated, may hold values from 0 to 15, never falling along the last dimension, each value on 1 to 256 neighbouring positions
- slabs: bfloat16 [4, 768, 3072], P('section'), as said below
- ffn_down: bfloat16 [2, 3072, 768], replicated, may hold values from -0.109375 to 0.109375
- ad_down: float32 [4, 768, 64], P('section'), may hold values from -0.21875 to 0.21875
- ad_down_bias: float32 [4, 64], P('section'), may hold values from -3 to 3
- ad_up: float32 [4, 64, 768], P('section'), may hold values from -0.75 to 0.75
- ad_up_bias: float32 [4, 768], P('section'), may hold values from -2 to 2
- ln_gain: float32 [4, 768], P('section'), may hold values from 0.5 to 1.5
- ln_bias: float32 [4, 768], P('section'), may hold values from -2 to 2
Outputs:
- block_outputs: bfloat16 [4, 8, 2048, 768], P('section', None, 'rows')
- input_grads: bfloat16 [4, 8, 2048, 768], P('section', None, 'rows')
- grad_ad_down: float32 [4, 768, 64], P('section')
- grad_ad_down_bias: float32 [4, 64], P('section')
- grad_ad_up: float32 [4, 64, 768], P('section')
- grad_ad_up_bias: float32 [4, 768], P('section')
- grad_ln_gain: float32 [4, 768], P('section')
- grad_ln_bias: float32 [4, 768], P('section')
Inputs may be any that keep to these rules, and one draw needn't show every extreme that they name: `segment_ids`: along each micro-batch the ids never fall; every id of 0 to 15 appears, each segment covers 1 to 256 rows and one covers exactly 256. For even b, columns 2304 to 3072 of slabs[b] are an output projection of larger entries than the other columns.
All inputs are finite; a program needn't handle non-finite values.
Results may differ from a plain program's by a relative error of at most 0.02.
Values may be sent and summed in bfloat16 or wider, within the bound.
No kernel may reach another device: no remote copies, remote signals or barrier semaphores. Data moves between devices by JAX's collectives and lax.ppermute only.
A program may use at most 192 MiB of HBM per device.

v0:
```python
import jax
import jax.numpy as jnp
from jax import lax
from jax.experimental import pallas as pl
from jax.experimental.pallas import tpu as pltpu
from jax.sharding import Mesh, PartitionSpec as P

HEADS = 12
GROUP = 2
PARTS = 4
EXTRA = 32
COST = 1e8
BF = jnp.bfloat16
F32 = jnp.float32
VMEM = pl.BlockSpec(memory_space=pltpu.VMEM)
ANY = pl.BlockSpec(memory_space=pl.ANY)
SMEM = pl.BlockSpec(memory_space=pltpu.SMEM)
LIMIT = 56 * 1024 * 1024


def dot(left, right):
    return jnp.dot(left, right, preferred_element_type=F32)


def dot_t(left, right):
    return lax.dot_general(left, right, (((1,), (1,)), ((), ())), preferred_element_type=F32)


def gelu_pair(x):
    size = jnp.abs(x)
    base = 1.0 + 0.23164188 * size
    t = 1.0 / base
    poly = 0.127414796 + t * (-0.142248368 + t * (0.710706871 + t * (
        -0.726576014 + t * 0.530702715)))
    bell = jnp.exp2(-0.7213475204444817 * (x * x))
    tail = (t * poly) * bell
    phi = jnp.where(x < 0, tail, 1.0 - tail)
    return x * phi, phi + x * (0.3989422804014327 * bell)


def like(shape, dtype=BF):
    return jax.ShapeDtypeStruct(shape, dtype)


def run(body, ins, outs, scratch, name, micros):
    n_in, n_out = len(ins), len(outs)

    def wrapped(*refs):
        body(refs[:n_in], refs[n_in : n_in + n_out], refs[n_in + n_out :])

    return pl.pallas_call(
        wrapped,
        out_shape=[shape for shape, _ in outs],
        in_specs=[spec for _, spec in ins],
        out_specs=[spec for _, spec in outs],
        scratch_shapes=scratch,
        name=name,
        cost_estimate=pl.CostEstimate(flops=int(micros * COST), bytes_accessed=0, transcendentals=0),
        compiler_params=pltpu.CompilerParams(vmem_limit_bytes=LIMIT),
    )(*[array for array, _ in ins])


class Group:
    def __init__(self, sems, count):
        self.sems, self.first, self.pairs = sems, sems.used, []
        sems.used += count

    def start(self, *pairs):
        for i, (source, target) in enumerate(pairs):
            pltpu.make_async_copy(source, target, self.sems.ref.at[self.first + i]).start()

    def wait(self, *pairs):
        for i, (source, target) in enumerate(pairs):
            pltpu.make_async_copy(source, target, self.sems.ref.at[self.first + i]).wait()


class Sems:
    def __init__(self, ref):
        self.ref, self.used = ref, 0

    def run(self, count):
        self.used += count
        return self.ref.at[pl.ds(self.used - count, count)]


def load_slab(sems, src, block, weights, slab_v):
    own, own_pack, bufs = weights
    rows = own.shape[0] // GROUP
    plane = src[block, GROUP + 2]
    for h in range(GROUP):
        for i, parts in enumerate([(own,)] + list(bufs)):
            size = rows // len(parts)

            @pl.when(src[block, h] == i)
            def _():
                for p in range(PARTS):
                    columns = pl.ds(p * (own.shape[1] // PARTS), own.shape[1] // PARTS)
                    for n, buf in enumerate(parts):
                        first = h * rows if i == 0 else 0
                        to = h * rows
                        if len(parts) > 1:
                            to += size * (plane if n == 0 else 1 - plane)
                        pltpu.make_async_copy(
                            buf.at[pl.ds(first, size), columns],
                            slab_v.at[pl.ds(pl.multiple_of(to, 64), size), columns],
                            sems.at[p]).start()


def slab_part(sems, weights, slab_v, p):
    own = weights[0]
    columns = part_of(own.shape[1], p)
    pltpu.make_async_copy(own.at[:, columns], slab_v.at[:, columns], sems.at[p]).wait()


def load_down(sems, down, layer, down_v):
    for p in range(PARTS):
        rows = pl.ds(p * (down_v.shape[0] // PARTS), down_v.shape[0] // PARTS)
        pltpu.make_async_copy(down.at[layer, rows], down_v.at[rows], sems.at[p]).start()


def down_part(sems, down, down_v, p):
    rows = part_of(down_v.shape[0], p)
    pltpu.make_async_copy(down.at[0, rows], down_v.at[rows], sems.at[p]).wait()


def load_pack(sem, src, block, weights, pack_v):
    own, own_pack, bufs = weights
    rows = own.shape[0] // GROUP
    size = own_pack.shape[0] // GROUP
    for h in range(GROUP):
        at = pl.ds(h * size, size)
        for i, parts in enumerate([(own_pack,)] + list(bufs)):
            buf = parts[0]
            first = h * size if i == 0 else rows // len(parts)

            @pl.when(src[block, h] == i)
            def _():
                pltpu.make_async_copy(buf.at[pl.ds(first, size)], pack_v.at[at], sem).start()


def send_grads(sem, value_ref, apart, outs):
    for d, out in enumerate(outs):
        @pl.when(apart == d)
        def _():
            pltpu.make_async_copy(value_ref, out, sem).start()


def row_copies(value_ref, block, core, out, sem):
    half = value_ref.shape[0] // GROUP
    return [pltpu.make_async_copy(
        value_ref.at[pl.ds(i * half, half)],
        out.at[GROUP * block + (core if i == 0 else GROUP - 1 - core)], sem) for i in range(GROUP)]


def adapters(pack, width, adapt):
    rows = [pack[:, i * width : (i + 1) * width] for i in range(2 * adapt // EXTRA)]
    zeros = jnp.zeros((128 - adapt, width), BF)
    per = adapt // EXTRA
    down_t = jnp.concatenate(rows[:per] + [zeros], axis=0)
    up = jnp.concatenate(rows[per:] + [zeros], axis=0)
    return down_t, up


def post_forward(pack, small, x_ref, b_ref, y_ref, saved, adapt):
    low_ref, ut_ref, slope_ref, zhat_ref, rstd_ref = saved
    rows, width = x_ref.shape
    down_t, up = adapters(pack, width, adapt)
    down_bias, up_bias, gain, bias = [small[i : i + 1, :] for i in range(4)]
    step = 512

    def body(i, carry):
        at = pl.ds(pl.multiple_of(i * step, step), step)
        branch = b_ref[at, :]
        low = branch.astype(BF)
        low_ref[at, :] = low
        pre = dot_t(low, down_t) + down_bias[:, :128]
        inner, slope = gelu_pair(pre)
        slope_ref[at, :] = slope
        ut_ref[:, at] = inner.T.astype(BF)
        mixed = x_ref[at, :].astype(F32) + branch + dot(inner.astype(BF), up) + up_bias
        center = mixed - jnp.mean(mixed, axis=-1, keepdims=True)
        rstd = lax.rsqrt(jnp.mean(center * center, axis=-1, keepdims=True) + 1e-05)
        zhat = center * rstd
        y_ref[at, :] = (zhat * gain + bias).astype(BF)
        zhat_ref[at, :] = zhat.astype(BF)
        rstd_ref[at, :] = jnp.broadcast_to(rstd, (step, 128))
        return carry

    lax.fori_loop(0, rows // step, body, 0)


def post_backward(pack, small, dy_ref, saved, dz_ref, db_ref, grads_ref, dpt_ref, adapt):
    low_ref, ut_ref, slope_ref, zhat_ref, rstd_ref = saved
    rows, width = dy_ref.shape
    down_t, up = adapters(pack, width, adapt)
    gain = small[2:3, :]
    step = 512

    def fold(v):
        return jnp.sum(v.reshape(v.shape[0] // 8, 8, v.shape[1]), axis=0)

    def body(i, carry):
        s_bias, s_gain, s_upb, s_downb = carry
        at = pl.ds(pl.multiple_of(i * step, step), step)
        d_out = dy_ref[at, :].astype(F32)
        zhat = zhat_ref[at, :].astype(F32)
        s_bias = s_bias + fold(d_out)
        s_gain = s_gain + fold(d_out * zhat)
        dz = d_out * gain
        dz = rstd_ref[at, :1] * (dz - jnp.mean(dz, axis=-1, keepdims=True)
                                 - zhat * jnp.mean(dz * zhat, axis=-1, keepdims=True))
        s_upb = s_upb + fold(dz)
        low = dz.astype(BF)
        db_ref[at, :] = low
        d_pre = dot_t(low, up) * slope_ref[at, :]
        s_downb = s_downb + fold(d_pre)
        dpt_ref[:, at] = d_pre.T.astype(BF)
        dz_ref[at, :] = dz
        return s_bias, s_gain, s_upb, s_downb

    zero = jnp.zeros((8, width), F32)
    s_bias, s_gain, s_upb, s_downb = lax.fori_loop(
        0, rows // step, body, (zero, zero, zero, jnp.zeros((8, 128), F32)))
    g_down = dot(dpt_ref[...], low_ref[...])
    g_up = dot(ut_ref[...], db_ref[...])
    grads_ref[0:adapt, :] = g_down[:adapt].astype(BF)
    grads_ref[adapt : 2 * adapt, :] = g_up[:adapt].astype(BF)
    tail = jnp.concatenate(
        [jnp.sum(v, axis=0, keepdims=True) for v in (s_upb, s_gain, s_bias)]
        + [jnp.concatenate([jnp.sum(s_downb, axis=0, keepdims=True),
                            jnp.zeros((1, width - 128), F32)], axis=1),
           jnp.zeros((EXTRA - 4, width), F32)], axis=0)
    grads_ref[2 * adapt :, :] = tail.astype(BF)

    def body2(i, carry):
        at = pl.ds(pl.multiple_of(i * step, step), step)
        d_pre = dpt_ref[:, at].astype(F32).T.astype(BF)
        db_ref[at, :] = (dz_ref[at, :] + dot(d_pre, down_t)).astype(BF)
        return carry

    lax.fori_loop(0, rows // step, body2, 0)


def tile(i, size):
    return pl.ds(pl.multiple_of(i * size, size), size)


def part_of(size, i):
    return tile(i, size // PARTS)


def ffn_branch(x_ref, slab, down, slope_ref, acc, ready, step=256):
    acc[...] = jnp.zeros_like(acc)
    size = slab.shape[1] // PARTS

    def part(i, carry):
        ready(i)
        act, before = None, None
        for j in range(size // step):
            cols = pl.ds(pl.multiple_of(i * size + j * step, step), step)
            values, slope = gelu_pair(dot(x_ref[...], slab[:, cols]))
            slope_ref[:, cols] = slope.astype(BF)
            if act is not None:
                acc[...] += dot(act, down[before, :])
            act, before = values.astype(BF), cols
        acc[...] += dot(act, down[before, :])
        return carry

    lax.fori_loop(0, PARTS, part, 0, unroll=2)


def ffn_branch_back(db, slab, down, slope_ref, acc, ready, step=256):
    size = slab.shape[1] // PARTS

    def part(i, carry):
        ready(i)
        df, before = None, None
        for j in range(size // step):
            cols = pl.ds(pl.multiple_of(i * size + j * step, step), step)
            dg = dot_t(db[...], down[cols, :])
            if df is not None:
                acc[...] += dot_t(df, slab[:, before])
            df, before = (dg * slope_ref[:, cols].astype(F32)).astype(BF), cols
        acc[...] += dot_t(df, slab[:, before])
        return carry

    lax.fori_loop(0, PARTS, part, 0, unroll=2)


def project(x_ref, slab, qkv_ref, ready, step=256):
    width = x_ref.shape[1]

    def part(i, carry):
        ready(i)
        scale = jnp.where(i == 0, (width // HEADS) ** -0.5, 1.0)
        for j in range(width // step):
            cols = pl.ds(pl.multiple_of(i * width + j * step, step), step)
            qkv_ref[:, cols] = (dot(x_ref[...], slab[:, cols]) * scale).astype(BF)
        return carry

    lax.fori_loop(0, 3, part, 0)


def attend(qkv_ref, bias_v, p_v, c_ref):
    rows, width = c_ref.shape
    head = width // HEADS
    lower = lax.broadcasted_iota(jnp.int32, (rows, 2 * head), 1) < head

    def body(i, carry):
        def part(n):
            return qkv_ref[:, pl.ds(pl.multiple_of(n * width + i * 2 * head, 2 * head), 2 * head)]

        q, k, v = part(0), part(1), part(2)
        parts = []
        for h in range(2):
            q_h = jnp.where(lower == (h == 0), q, jnp.zeros_like(q))
            s = dot_t(q_h, k) + bias_v[...]
            e = jnp.exp(s - jnp.max(s, axis=-1, keepdims=True))
            p = (e * (1.0 / jnp.sum(e, axis=-1, keepdims=True))).astype(BF)
            p_v[2 * i + h] = p
            parts.append(dot(p, v))
        c_ref[:, tile(i, 2 * head)] = jnp.where(lower, parts[0], parts[1]).astype(BF)
        return carry

    lax.fori_loop(0, HEADS // 2, body, 0, unroll=6)


def attend_back(qkv_ref, c_ref, dc_ref, p_v, dqkv):
    rows, width = c_ref.shape
    head = width // HEADS
    lower = lax.broadcasted_iota(jnp.int32, (rows, 2 * head), 1) < head

    def body(i, carry):
        def cols(n):
            return pl.ds(pl.multiple_of(n * width + i * 2 * head, 2 * head), 2 * head)

        q, k, v = qkv_ref[:, cols(0)], qkv_ref[:, cols(1)], qkv_ref[:, cols(2)]
        dc = dc_ref[:, cols(0)]
        dc_wide = dc.astype(F32)
        prod = dc_wide * c_ref[:, cols(0)].astype(F32)
        q_t = q.astype(F32).T.astype(BF)
        dc_t = dc_wide.T.astype(BF)
        dq, dk, dv = [], [], []
        for h in range(2):
            mine = lower == (h == 0)
            p = p_v[2 * i + h]
            delta = jnp.sum(jnp.where(mine, prod, 0.0), axis=-1, keepdims=True)
            dp = dot_t(jnp.where(mine, dc, jnp.zeros_like(dc)), v)
            ds = (p.astype(F32) * (dp - delta)).astype(BF)
            dq.append(dot(ds, k))
            dk.append(dot(q_t[h * head : (h + 1) * head], ds))
            dv.append(dot(dc_t[h * head : (h + 1) * head], p))
        dqkv[:, cols(0)] = (jnp.where(lower, dq[0], dq[1]) * head ** -0.5).astype(BF)
        dqkv[:, cols(1)] = jnp.concatenate(dk, axis=0).T.astype(BF)
        dqkv[:, cols(2)] = jnp.concatenate(dv, axis=0).T.astype(BF)
        return carry

    lax.fori_loop(0, HEADS // 2, body, 0, unroll=6)


def by_columns(target, value, step=256):
    for j in range(target.shape[1] // step):
        cols = slice(j * step, (j + 1) * step)
        target[:, cols] = value(cols).astype(target.dtype)


def post_saved(rows, width):
    return [((rows, width), BF), ((128, rows), BF), ((rows, 128), F32), ((rows, width), BF),
            ((rows, 128), F32)]


def block_saved(block, rows, width, ff):
    if block % 2 == 0:
        first = [((rows, 3 * width), BF), ((rows, width), BF), ((HEADS, rows, rows), BF)]
    else:
        first = [((rows, ff), BF)]
    return first + post_saved(rows, width)


def weight_ins(weights):
    own, own_pack, bufs = weights
    return [(own, ANY), (own_pack, ANY)] + [(x, ANY) for parts in bufs for x in parts]


def weight_refs(refs, weights):
    refs, parts = list(refs), []
    for group in weights[2]:
        parts.append(tuple(refs[2 + sum(map(len, parts)) :][: len(group)]))
    return refs[0], refs[1], parts


def forward(x, seg, src, weights, small, down, adapt):
    rows, width = x.shape
    ff = weights[0].shape[1]
    layers = down.shape[0]
    n_w = len(weight_ins(weights))
    shapes = [block_saved(b, rows, width, ff) for b in range(2)]
    n_a = len(shapes[0])

    def body(ins, outs, scratch):
        src_ref, x_ref, segc_ref, segr_ref, small_ref, down_ref = ins[:6]
        wts = weight_refs(ins[6 : 6 + n_w], weights)
        out_a, out_f, sent = outs[:n_a], outs[n_a:-1], outs[-1]
        slabs, packs, down_v, y_v, acc, bias_v, sem_ref = scratch[:7]
        buf_a, buf_f = scratch[7 : 7 + n_a], scratch[7 + n_a :]
        sems = Sems(sem_ref)
        slab_sems = [sems.run(PARTS) for b in range(2)]
        down_sems, pack_sem = sems.run(PARTS), sems.run(1).at[0]
        group_a, group_f = Group(sems, n_a), Group(sems, len(buf_f))
        rows_sems = sems.run(2)
        core = src_ref[0, GROUP + 1]

        load_slab(slab_sems[0], src_ref, 0, wts, slabs.at[0])
        for b in range(2 * layers):
            load_pack(pack_sem, src_ref, b, wts, packs.at[b])
        bias_v[...] = jnp.where(segc_ref[...] == segr_ref[...], 0.0, -1e30)
        y_v[1] = x_ref[...]
        for b in range(2 * layers):
            pltpu.make_async_copy(wts[1], packs.at[b], pack_sem).wait()

        def save_a(layer):
            return [(buf, out.at[layer]) for buf, out in zip(buf_a, out_a)]

        def save_f(layer):
            return [(buf, out.at[layer]) for buf, out in zip(buf_f, out_f)]

        def wait_rows(i):
            for copy in row_copies(y_v.at[i], 0, 0, sent, rows_sems.at[i]):
                copy.wait()

        def layer_step(layer, carry):
            b = 2 * layer
            slab = slabs.at[0]

            @pl.when(layer > 0)
            def _():
                group_a.wait(*save_a(0))
                wait_rows(0)

            qkv, ctx, probs = buf_a[:3]
            project(y_v.at[1], slab, qkv, lambda i: slab_part(slab_sems[0], wts, slab, i))
            slab_part(slab_sems[0], wts, slab, PARTS - 1)
            load_slab(slab_sems[1], src_ref, b + 1, wts, slabs.at[1])
            load_down(down_sems, down_ref, layer, down_v)
            attend(qkv, bias_v, probs, ctx)
            by_columns(acc, lambda cols: dot(
                ctx[...], slab[:, 3 * width + cols.start : 3 * width + cols.stop]))

            @pl.when(layer + 1 < layers)
            def _():
                load_slab(slab_sems[0], src_ref, b + 2, wts, slab)

            post_forward(packs.at[b], small_ref.at[src_ref[b, GROUP]], y_v.at[1], acc, y_v.at[0],
                         buf_a[3:], adapt)
            for copy in row_copies(y_v.at[0], b, core, sent, rows_sems.at[0]):
                copy.start()
            group_a.start(*save_a(layer))

            @pl.when(layer > 0)
            def _():
                group_f.wait(*save_f(0))
                wait_rows(1)

            def ready(i):
                slab_part(slab_sems[1], wts, slabs.at[1], i)
                down_part(down_sems, down_ref, down_v, i)

            ffn_branch(y_v.at[0], slabs.at[1], down_v, buf_f[0], acc, ready)
            post_forward(packs.at[b + 1], small_ref.at[src_ref[b + 1, GROUP]], y_v.at[0], acc,
                         y_v.at[1], buf_f[1:], adapt)
            for copy in row_copies(y_v.at[1], b + 1, core, sent, rows_sems.at[1]):
                copy.start()
            group_f.start(*save_f(layer))
            return carry

        lax.fori_loop(0, layers, layer_step, 0)
        group_a.wait(*save_a(0))
        group_f.wait(*save_f(0))
        for i in range(2):
            wait_rows(i)

    outs = [(like((layers,) + sh, dt), ANY) for b in range(2) for sh, dt in shapes[b]]
    outs.append((like((2 * layers * GROUP, rows // GROUP, width)), ANY))
    scratch = [
        pltpu.VMEM((2,) + weights[0].shape, BF),
        pltpu.VMEM((2 * layers,) + weights[1].shape, BF),
        pltpu.VMEM((ff, width), BF), pltpu.VMEM((2, rows, width), BF),
        pltpu.VMEM((rows, width), F32), pltpu.VMEM((rows, rows), F32),
        pltpu.SemaphoreType.DMA((48,))]
    for b in range(2):
        scratch += [pltpu.VMEM(sh, dt) for sh, dt in shapes[b]]
    res = run(
        body, [(src, SMEM), (x, VMEM), (seg[:, None], VMEM), (seg[None, :], VMEM), (small, VMEM),
               (down, ANY)] + weight_ins(weights), outs, scratch, "forward", 60)
    return (res[:n_a], res[n_a:-1]), res[-1]


def backward(dy, saved, src, weights, small, down, adapt):
    rows, width = dy.shape
    ff = weights[0].shape[1]
    layers = down.shape[0]
    n_w = len(weight_ins(weights))
    saved_a, saved_f = saved
    n_a, n_f = len(saved_a), len(saved_f)

    def body(ins, outs, scratch):
        src_ref, dy_ref, small_ref, down_ref = ins[:4]
        wts = weight_refs(ins[4 : 4 + n_w], weights)
        in_a, in_f = ins[4 + n_w : 4 + n_w + n_a], ins[4 + n_w + n_a :]
        sent, grads_out = outs[0], outs[1:]
        slabs, packs, down_v, acc, db, dpt, grads, dx_v, dc_v, dqkv, dy_v, sem_ref = scratch[:12]
        buf_a, buf_f = scratch[12 : 12 + n_a], scratch[12 + n_a :]
        sems = Sems(sem_ref)
        slab_sems = [sems.run(PARTS) for i in range(2)]
        down_sems, pack_sems = sems.run(PARTS), sems.run(2)
        group_a, group_f, group_dy = Group(sems, n_a), Group(sems, n_f), Group(sems, 1)
        rows_sems, grads_sems = sems.run(2), sems.run(2)
        core = src_ref[0, GROUP + 1]

        def load_a(layer):
            return [(x.at[layer], buf) for x, buf in zip(in_a[3:] + in_a[:3], buf_a[3:] + buf_a[:3])]

        def load_f(layer):
            return [(x.at[layer], buf) for x, buf in zip(in_f[1:] + in_f[:1], buf_f[1:] + buf_f[:1])]

        def fetch_f(layer):
            b = 2 * layer + 1
            group_f.start(*load_f(layer))
            load_pack(pack_sems.at[0], src_ref, b, wts, packs.at[0])
            load_down(down_sems, down_ref, layer, down_v)
            load_slab(slab_sems[0], src_ref, b, wts, slabs.at[0])

        def wait_pack(i):
            pltpu.make_async_copy(wts[1], packs.at[i], pack_sems.at[i]).wait()

        def wait_sent(i, value_ref):
            for copy in row_copies(value_ref, 0, 0, sent, rows_sems.at[i]):
                copy.wait()
            pltpu.make_async_copy(grads.at[i], grads_out[0], grads_sems.at[i]).wait()

        group_dy.start((dy_ref, dy_v))
        fetch_f(layers - 1)
        group_dy.wait((dy_ref, dy_v))

        def layer_step(count, carry):
            layer = layers - 1 - count
            b = 2 * layer + 1

            @pl.when(count > 0)
            def _():
                wait_sent(0, dx_v)

            group_f.wait(*load_f(0))
            wait_pack(0)
            post_backward(packs.at[0], small_ref.at[src_ref[b, GROUP]], dy_v, buf_f[1:], acc, db,
                          grads.at[0], dpt, adapt)
            send_grads(grads_sems.at[0], grads.at[0], src_ref[b, GROUP], grads_out)
            load_pack(pack_sems.at[1], src_ref, b - 1, wts, packs.at[1])
            group_a.start(*load_a(layer))
            load_slab(slab_sems[1], src_ref, b - 1, wts, slabs.at[1])

            def ready(i):
                slab_part(slab_sems[0], wts, slabs.at[0], i)
                down_part(down_sems, down_ref, down_v, i)

            ffn_branch_back(db, slabs.at[0], down_v, buf_f[0], acc, ready)
            dx_v[...] = acc[...].astype(BF)
            for copy in row_copies(dx_v, b, core, sent, rows_sems.at[0]):
                copy.start()

            @pl.when(count > 0)
            def _():
                wait_sent(1, dy_v)

            group_a.wait(*load_a(0))
            wait_pack(1)

            @pl.when(layer > 0)
            def _():
                fetch_f(layer - 1)

            post_backward(packs.at[1], small_ref.at[src_ref[b - 1, GROUP]], dx_v, buf_a[3:], acc,
                          db, grads.at[1], dpt, adapt)
            send_grads(grads_sems.at[1], grads.at[1], src_ref[b - 1, GROUP], grads_out)
            slab = slabs.at[1]
            for i in range(PARTS):
                slab_part(slab_sems[1], wts, slab, i)
            by_columns(dc_v, lambda cols: dot_t(db[...], slab[cols, 3 * width :]))
            attend_back(buf_a[0], buf_a[1], dc_v, buf_a[2], dqkv)
            by_columns(dy_v, lambda cols: acc[:, cols] + dot_t(dqkv[...], slab[cols, : 3 * width]))
            for copy in row_copies(dy_v, b - 1, core, sent, rows_sems.at[1]):
                copy.start()
            return carry

        lax.fori_loop(0, layers, layer_step, 0)
        wait_sent(0, dx_v)
        wait_sent(1, dy_v)

    grad_shape = (2 * adapt + EXTRA, width)
    outs = [(like((2 * layers * GROUP, rows // GROUP, width)), ANY)]
    outs += [(like(grad_shape), ANY)] * (2 * layers)
    scratch = [
        pltpu.VMEM((2,) + weights[0].shape, BF), pltpu.VMEM((2,) + weights[1].shape, BF),
        pltpu.VMEM((ff, width), BF), pltpu.VMEM((rows, width), F32), pltpu.VMEM((rows, width), BF),
        pltpu.VMEM((128, rows), BF), pltpu.VMEM((2,) + grad_shape, BF),
        pltpu.VMEM((rows, width), BF), pltpu.VMEM((rows, width), BF),
        pltpu.VMEM((rows, 3 * width), BF), pltpu.VMEM((rows, width), BF),
        pltpu.SemaphoreType.DMA((48,))]
    scratch += [pltpu.VMEM(x.shape[1:], x.dtype) for x in tuple(saved_a) + tuple(saved_f)]
    res = run(
        body, [(src, SMEM), (dy, ANY), (small, VMEM), (down, ANY)] + weight_ins(weights)
        + [(x, ANY) for x in tuple(saved_a) + tuple(saved_f)], outs, scratch, "backward", 60)
    return res[0], res[1:]


def settle(x):
    def body(ins, outs, scratch):
        buf, sems = scratch
        loads = [pltpu.make_async_copy(ins[0].at[i], buf.at[i], sems.at[i])
                 for i in range(x.shape[0])]
        stores = [pltpu.make_async_copy(buf.at[i], outs[0].at[i], sems.at[i])
                  for i in range(x.shape[0])]
        for load in loads:
            load.start()
        for load, store in zip(loads, stores):
            load.wait()
            store.start()
        for store in stores:
            store.wait()

    return run(body, [(x, ANY)], [(like(x.shape), ANY)],
               [pltpu.VMEM(x.shape, BF), pltpu.SemaphoreType.DMA((x.shape[0],))], "settle", 3)[0]


def per_device(tokens, cotangent, segment_ids, slabs, ffn_down,
               ad_down, ad_down_bias, ad_up, ad_up_bias, ln_gain, ln_bias):
    n_section, n_group = lax.axis_size("section"), lax.axis_size("group")
    s, group, core = (lax.axis_index(name) for name in ("section", "group", "core"))
    n_micro, rows_dev, width = tokens.shape
    adapt = ad_down.shape[2]
    sections = range(n_section)

    def sect(x, apart):
        return lax.ppermute(x, "section", [(i, i ^ apart) for i in sections])

    def peer(x):
        return lax.ppermute(x, "core", [(0, 1), (1, 0)])

    def by_core(x, apart):
        pairs = [(i * GROUP + c, (i ^ apart[c]) * GROUP + c) for i in sections for c in range(GROUP)]
        return lax.ppermute(x, ("section", "core"), pairs)

    slab = slabs[0]
    half = slab.shape[0] // GROUP
    mats = jnp.concatenate([ad_down[0].T, ad_up[0]], axis=0).astype(BF)
    own_pack = jnp.concatenate([mats[i : i + EXTRA] for i in range(0, 2 * adapt, EXTRA)], axis=1)
    own_small = jnp.concatenate([jnp.pad(ad_down_bias, ((0, 0), (0, width - adapt))), ad_up_bias,
                                 ln_gain, ln_bias, jnp.zeros((4, width), F32)], axis=0)
    small = [own_small] + [sect(own_small, d) for d in range(1, n_section)]
    size = own_pack.shape[0] // GROUP
    plane = group % 2
    pack_half = lax.dynamic_slice_in_dim(own_pack, core * size, size, 0)
    quarter = lax.dynamic_slice_in_dim(slab, core * half + plane * (half // 2), half // 2, 0)
    given = jnp.concatenate([lax.dynamic_slice_in_dim(slab, core * half, half, 0), pack_half],
                            axis=0)
    own_micro = s * GROUP + core
    peer_micro = s * GROUP + 1 - core

    def gather_item(x):
        mine = lax.dynamic_index_in_dim(x, own_micro, 0, keepdims=False)
        given = lax.dynamic_index_in_dim(x, peer_micro, 0, keepdims=False)
        return jnp.concatenate([mine, peer(given)], axis=0)

    hidden = gather_item(tokens)
    cot = gather_item(cotangent)
    second = by_core(given, (2, 1))
    first = by_core(jnp.concatenate([quarter, pack_half], axis=0), (1, 2))
    second, first, hidden, cot, *small = lax.optimization_barrier(
        (second, first, hidden, cot, *small))
    first_z = lax.ppermute(first, "group", [(i, i ^ 1) for i in range(n_group)])
    third = by_core(second, (1, 2))
    bufs = [(first, first_z), (second,), (third,)]
    bufs += [tuple(peer(x) for x in parts) for parts in bufs]
    small = jnp.stack(small)

    item_start = group * GROUP * rows_dev
    seg = jnp.concatenate([
        lax.dynamic_slice(segment_ids, (own_micro, item_start + c * rows_dev), (1, rows_dev))[0]
        for c in (core, 1 - core)])

    def source(b):
        d = s ^ b
        at = []
        for h in range(GROUP):
            i = jnp.where(d == 3, 3, jnp.where((d == 1) == (h == 0), 1, 2))
            at.append(jnp.where(d == 0, 0, jnp.where(core == h, i, i + 3)))
        return jnp.stack(at + [d, core, plane]).astype(jnp.int32)

    src = jnp.stack([source(b) for b in sections])
    weights = (slab, own_pack, bufs)

    def to_owners(x):
        return lax.all_to_all(x, ("section", "core"), 0, 0, tiled=True)

    saved, sent = forward(hidden, seg, src, weights, small, ffn_down, adapt)
    block_outputs = to_owners(sent)
    leaving, grads = backward(cot, saved, src, weights, small, ffn_down, adapt)
    block_outputs, leaving, *grads = lax.optimization_barrier((block_outputs, leaving, *grads))
    block_outputs = settle(block_outputs)

    coming = [sect(grads[d], d) for d in range(1, n_section)]
    *coming, leaving = lax.optimization_barrier((*coming, leaving))
    total = grads[0].astype(F32)
    for part in coming:
        total = total + part.astype(F32)
    total = total.astype(BF)
    input_grads = to_owners(leaving)
    total = (total.astype(F32) + peer(total).astype(F32)).astype(BF)
    apart = 1
    while apart < n_group:
        other = lax.ppermute(total, "group", [(i, i ^ apart) for i in range(n_group)])
        total = (total.astype(F32) + other.astype(F32)).astype(BF)
        apart *= 2
    total = total.astype(F32)
    return (block_outputs[None], input_grads[None], total[:adapt].T[None],
            total[2 * adapt + 3, :adapt][None], total[adapt : 2 * adapt][None],
            total[2 * adapt][None], total[2 * adapt + 1][None], total[2 * adapt + 2][None])


def solution(mesh):
    n_section, n_rows = mesh.devices.shape
    cores = Mesh(mesh.devices.reshape(n_section, n_rows // GROUP, GROUP),
                 ("section", "group", "core"))
    rows = ("group", "core")
    in_specs = (
        P(None, rows, None), P(None, rows, None), P(), P("section", None, None), P(),
        P("section", None, None), P("section", None), P("section", None, None),
        P("section", None), P("section", None), P("section", None),
    )
    out_specs = (
        P("section", None, rows, None), P("section", None, rows, None),
        P("section", None, None), P("section", None), P("section", None, None),
        P("section", None), P("section", None), P("section", None),
    )
    return jax.shard_map(
        per_device, mesh=cores, in_specs=in_specs, out_specs=out_specs, check_vma=False
    )
```

profile of v0, /device:TPU:0, one launch (start us, length us, event | category | flops | bytes accessed | tf_op | source)
XLA Modules:
  0.0 246.5 jit_solution(1882072818725275489)
XLA Ops:
  0.6 0.9 convert.10
  1.6 0.9 convert_bitcast_fusion
  2.6 0.0 copy-start.2
  2.6 1.9 dynamic-slice_bitcast_fusion
  4.5 1.6 pad_maximum_fusion
  6.1 3.0 %collective-permute-start = (bf16[400,3072]{1,0:T(8,128)(2,1)}, bf16[400,3072]{1,0:T(8,128)(2,1)S(1)}, u32[]{:S(2)}, u32[]{:S(2)}) collective-permute-start(bf16[400,3072]{1,0:T(8,128)(2,1)} %pad_maximum_fusion), channel_id=1, source_target_pairs={{0,16},{1,9},{8,24},{9,1},{16,0},{17,25},{24,8},{25,17},{2,18},{3,... | collective-permute-start | bytes 7372808 | tf_op jit(solution)/shard_map/ppermute | solution.py:651
  9.1 1.3 dynamic-slice_bitcast_fusion.1
  10.4 0.0 copy-start.8
  10.4 0.0 copy-start.5
  10.4 0.0 copy-start.6
  10.5 0.0 copy-start.7
  10.5 1.1 pad_maximum_fusion.1
  11.6 1.5 collective-permute-start.1
  13.1 2.0 dynamic-slice_bitcast_fusion.5
  15.1 1.9 dynamic-slice_bitcast_fusion.3
  17.0 0.5 collective-permute-start.3
  17.6 0.6 collective-permute-start.4
  18.2 0.1 collective-permute-start.5
  18.2 1.9 pad_maximum_fusion.2.refs_1_
  20.2 2.9 %collective-permute-start.6 = (f32[8,768]{1,0:T(8,128)S(1)}, f32[8,768]{1,0:T(8,128)S(1)}, u32[]{:S(2)}, u32[]{:S(2)}) collective-permute-start(f32[8,768]{1,0:T(8,128)S(1)} %concatenate.28), channel_id=1, source_target_pairs={{0,24},{8,16},{16,8},{24,0},{1,25},{9,17},{17,9},{25,1},{2,26},{10... | collective-permute-start | bytes 73736 | tf_op jit(solution)/shard_map/ppermute | solution.py:644
  23.1 1.9 pad_maximum_fusion.3.refs_1_
  25.0 18.4 %collective-permute-done.4 = f32[8,768]{1,0:T(8,128)S(1)} collective-permute-done((f32[8,768]{1,0:T(8,128)S(1)}, f32[8,768]{1,0:T(8,128)S(1)}, u32[]{:S(2)}, u32[]{:S(2)}) %collective-permute-start.4) | collective-permute-done | bytes 24608 | tf_op jit(solution)/shard_map/ppermute | solution.py:644
  43.4 8.3 %collective-permute-done.5 = f32[8,768]{1,0:T(8,128)S(1)} collective-permute-done((f32[8,768]{1,0:T(8,128)S(1)}, f32[8,768]{1,0:T(8,128)S(1)}, u32[]{:S(2)}, u32[]{:S(2)}) %collective-permute-start.5) | collective-permute-done | bytes 24608 | tf_op jit(solution)/shard_map/ppermute | solution.py:644
  51.7 0.0 copy-start.1
  51.7 2.3 collective-permute-start.8
  54.0 1.6 collective-permute-start.7
  55.6 26.4 %collective-permute-done.8.refs_11_.refs_9_ = bf16[400,3072]{1,0:T(8,128)(2,1)} collective-permute-done((bf16[400,3072]{1,0:T(8,128)(2,1)S(1)}, bf16[400,3072]{1,0:T(8,128)(2,1)}, u32[]{:S(2)}, u32[]{:S(2)}) %collective-permute-start.8) | collective-permute-done | bytes 2457632 | tf_op jit(solution)/shard_map/ppermute | solution.py:651
  82.0 0.5 collective-permute-start.9
  82.5 0.3 collective-permute-done.7.refs_9_.refs_7_
  82.8 0.8 fusion.3
  83.6 0.9 copy.19.refs_2_
  84.5 0.1 stack.110
  84.6 0.1 stack.105
  84.6 0.1 stack.100
  84.7 0.1 stack.95
  84.8 0.6 pad_add_fusion.refs_0_
  85.4 0.6 pad_maximum_fusion.5.refs_4_.refs_2_
  86.1 2.8 %collective-permute-done.9.refs_12_.refs_10_ = bf16[208,3072]{1,0:T(8,128)(2,1)} collective-permute-done((bf16[208,3072]{1,0:T(8,128)(2,1)}, bf16[208,3072]{1,0:T(8,128)(2,1)}, u32[]{:S(2)}, u32[]{:S(2)}) %collective-permute-start.9) | collective-permute-done | bytes 1277984 | tf_op jit(solution)/shard_map/ppermute | solution.py:647
  88.8 1.8 collective-permute-done.10.refs_13_.refs_11_
  90.7 47.3 %forward.1 = (bf16[2,512,2304]{2,1,0:T(8,128)(2,1)}, bf16[2,512,768]{2,1,0:T(8,128)(2,1)}, bf16[2,12,512,512]{3,2,1,0:T(8,128)(2,1)}, bf16[2,512,768]{2,1,0:T(8,...) custom-call(s32[4,5]{1,0:T(4,128)} %pad_add_fusion.refs_0_, ...), custom_call_target="tpu_custom_call" | custom-call | flops 6000000000 | tf_op jit(solution)/shard_map/forward/pallas_call | solution.py:51
  138.0 4.3 %all-to-all-start = ((bf16[8,256,768]{2,1,0:T(8,128)(2,1)}), bf16[8,256,768]{2,1,0:T(8,128)(2,1)S(1)}, u32[]{:S(2)}, u32[]{:S(2)}) async-start(bf16[8,256,768]{2,1,0:T(8,128)(2,1)} %get-tuple-element.53), calls=%async_computation | async-start | bytes 6291456 | tf_op jit(solution)/shard_map/all_to_all | solution.py:703
  142.3 42.7 %backward.1 = (bf16[8,256,768]{2,1,0:T(8,128)(2,1)}, bf16[160,768]{1,0:T(8,128)(2,1)}, bf16[160,768]{1,0:T(8,128)(2,1)}, bf16[160,768]{1,0:T(8,128)(2,1)}, bf16[160,768]{1,0:T(8,128)(2,1)}) custom-call(s32[4,5]{1,0:T(4,128)} %pad_add_fusion.refs_0_, bf16[512,768]{1,0:T(8,128)(2,1)} %pad_maximum_fusion.3.refs_1_, ...), custom_call_target="tpu_custom_call" | custom-call | flops 6000000000 | tf_op jit(solution)/shard_map/backward/pallas_call | solution.py:51
  185.0 2.1 collective-permute-start.13
  187.1 1.5 collective-permute-start.14
  188.6 0.1 collective-permute-start.15
  188.6 5.5 %collective-permute-done.13 = bf16[160,768]{1,0:T(8,128)(2,1)} collective-permute-done((bf16[160,768]{1,0:T(8,128)(2,1)}, bf16[160,768]{1,0:T(8,128)(2,1)}, u32[]{:S(2)}, u32[]{:S(2)}) %collective-permute-start.13) | collective-permute-done | bytes 245792 | tf_op jit(solution)/shard_map/ppermute | solution.py:644
  194.1 6.2 %collective-permute-done.14 = bf16[160,768]{1,0:T(8,128)(2,1)} collective-permute-done((bf16[160,768]{1,0:T(8,128)(2,1)}, bf16[160,768]{1,0:T(8,128)(2,1)}, u32[]{:S(2)}, u32[]{:S(2)}) %collective-permute-start.14) | collective-permute-done | bytes 245792 | tf_op jit(solution)/shard_map/ppermute | solution.py:644
  200.4 4.5 %all-to-all-start.1 = ((bf16[8,256,768]{2,1,0:T(8,128)(2,1)}), bf16[8,256,768]{2,1,0:T(8,128)(2,1)}, u32[]{:S(2)}, u32[]{:S(2)}) async-start(bf16[8,256,768]{2,1,0:T(8,128)(2,1)} %get-tuple-element.79), calls=%async_computation.1 | async-start | bytes 6291456 | tf_op jit(solution)/shard_map/all_to_all | solution.py:703
  204.8 1.3 add_convert_fusion.3
  206.1 0.4 collective-permute-start.16
  206.6 1.1 collective-permute-done.16
  207.7 0.1 add_convert_fusion.2
  207.8 1.7 collective-permute-start.17
  209.4 6.6 %collective-permute-done.17 = bf16[160,768]{1,0:T(8,128)(2,1)S(1)} collective-permute-done((bf16[160,768]{1,0:T(8,128)(2,1)S(1)}, bf16[160,768]{1,0:T(8,128)(2,1)S(1)}, u32[]{:S(2)}, u32[]{:S(2)}) %collective-permute-start.17) | collective-permute-done | bytes 245792 | tf_op jit(solution)/shard_map/ppermute | solution.py:721
  216.1 0.1 add_convert_fusion.1
  216.1 2.6 %collective-permute-start.18 = (bf16[160,768]{1,0:T(8,128)(2,1)S(1)}, bf16[160,768]{1,0:T(8,128)(2,1)S(1)}, u32[]{:S(2)}, u32[]{:S(2)}) collective-permute-start(bf16[160,768]{1,0:T(8,128)(2,1)S(1)} %add_convert_fusion.1), channel_id=1, source_target_pairs={{0,4},{2,6},{4,0},{6,2},{1,5},{3,7},{5,1},{7,3},{8,12},{10,14},{12... | collective-permute-start | bytes 737288 | tf_op jit(solution)/shard_map/ppermute | solution.py:721
  218.8 2.7 %settle.1 = bf16[8,256,768]{2,1,0:T(8,128)(2,1)} custom-call(bf16[8,256,768]{2,1,0:T(8,128)(2,1)} %copy-done), custom_call_target="tpu_custom_call" | custom-call | flops 300000000 | tf_op jit(solution)/shard_map/settle/pallas_call | solution.py:51
  221.5 8.4 %collective-permute-done.18 = bf16[160,768]{1,0:T(8,128)(2,1)S(1)} collective-permute-done((bf16[160,768]{1,0:T(8,128)(2,1)S(1)}, bf16[160,768]{1,0:T(8,128)(2,1)S(1)}, u32[]{:S(2)}, u32[]{:S(2)}) %collective-permute-start.18) | collective-permute-done | bytes 245792 | tf_op jit(solution)/shard_map/ppermute | solution.py:721
  229.9 0.1 fusion
  229.9 0.5 slice.57
  230.5 0.6 fusion.1
  231.0 0.8 slice_bitcast_fusion
  231.8 10.9 %all-to-all-done.1 = bf16[8,256,768]{2,1,0:T(8,128)(2,1)} async-done(((bf16[8,256,768]{2,1,0:T(8,128)(2,1)}), bf16[8,256,768]{2,1,0:T(8,128)(2,1)}, u32[]{:S(2)}, u32[]{:S(2)}) %all-to-all-start.1) | async-done | bytes 3145760 | tf_op jit(solution)/shard_map/all_to_all | solution.py:703
  242.7 3.8 %copy.21 = bf16[1,8,256,768]{3,2,1,0:T(8,128)(2,1)} copy(bf16[1,8,256,768]{3,2,1,0:T(8,128)(2,1)} %bitcast.39) | data formatting | bytes 6291456
  (33 shorter events, 0.2 us)
Async XLA Ops:
  2.6 1.9 copy-start.2
  6.1 45.5 %collective-permute-start = (bf16[400,3072]{1,0:T(8,128)(2,1)}, bf16[400,3072]{1,0:T(8,128)(2,1)S(1)}, u32[]{:S(2)}, u32[]{:S(2)}) collective-permute-start(bf16[400,3072]{1,0:T(8,128)(2,1)} %pad_maximum_fusion), channel_id=1, source_target_pairs={{0,16},{1,9},{8,24},{9,1},{16,0},{17,25},{24,8},{25,17},{2,18},{3,... | collective-permute-start | bytes 7372808 | tf_op jit(solution)/shard_map/ppermute | solution.py:651
  10.4 7.1 %copy-start.8 = (f32[1,64]{1,0:T(1,128)S(1)}, f32[1,64]{1,0:T(1,128)}, u32[]{:S(2)}) copy-start(f32[1,64]{1,0:T(1,128)} %param.17) | copy-start | bytes 772
  10.4 7.1 %copy-start.5 = (f32[1,768]{1,0:T(1,128)S(1)}, f32[1,768]{1,0:T(1,128)}, u32[]{:S(2)}) copy-start(f32[1,768]{1,0:T(1,128)} %param.19) | copy-start | bytes 9220
  10.4 7.1 %copy-start.6 = (f32[1,768]{1,0:T(1,128)S(1)}, f32[1,768]{1,0:T(1,128)}, u32[]{:S(2)}) copy-start(f32[1,768]{1,0:T(1,128)} %param.20) | copy-start | bytes 9220
  10.5 7.1 %copy-start.7 = (f32[1,768]{1,0:T(1,128)S(1)}, f32[1,768]{1,0:T(1,128)}, u32[]{:S(2)}) copy-start(f32[1,768]{1,0:T(1,128)} %param.21) | copy-start | bytes 9220
  11.6 40.0 %collective-permute-start.1 = (bf16[208,3072]{1,0:T(8,128)(2,1)}, bf16[208,3072]{1,0:T(8,128)(2,1)}, u32[]{:S(2)}, u32[]{:S(2)}) collective-permute-start(bf16[208,3072]{1,0:T(8,128)(2,1)} %pad_maximum_fusion.1), channel_id=1, source_target_pairs={{0,8},{1,17},{8,0},{9,25},{16,24},{17,1},{24,16},{25,9},{2,10},{3,... | collective-permute-start | bytes 3833864 | tf_op jit(solution)/shard_map/ppermute | solution.py:651
  15.1 3.1 %collective-permute-start.2 = (bf16[256,768]{1,0:T(8,128)(2,1)}, bf16[256,768]{1,0:T(8,128)(2,1)}, u32[]{:S(2)}, u32[]{:S(2)}) collective-permute-start(bf16[256,768]{1,0:T(8,128)(2,1)} %get-tuple-element.87), channel_id=1, source_target_pairs={{0,1},{1,0},{2,3},{3,2},{4,5},{5,4},{6,7},{7,6},{8,9},{9,8},{10,11... | collective-permute-start | bytes 1179656 | tf_op jit(solution)/shard_map/ppermute | solution.py:647
  17.0 3.2 %collective-permute-start.3 = (bf16[256,768]{1,0:T(8,128)(2,1)}, bf16[256,768]{1,0:T(8,128)(2,1)}, u32[]{:S(2)}, u32[]{:S(2)}) collective-permute-start(bf16[256,768]{1,0:T(8,128)(2,1)} %get-tuple-element.85), channel_id=1, source_target_pairs={{0,1},{1,0},{2,3},{3,2},{4,5},{5,4},{6,7},{7,6},{8,9},{9,8},{10,11... | collective-permute-start | bytes 1179656 | tf_op jit(solution)/shard_map/ppermute | solution.py:647
  17.6 25.8 %collective-permute-start.4 = (f32[8,768]{1,0:T(8,128)S(1)}, f32[8,768]{1,0:T(8,128)S(1)}, u32[]{:S(2)}, u32[]{:S(2)}) collective-permute-start(f32[8,768]{1,0:T(8,128)S(1)} %concatenate.28), channel_id=1, source_target_pairs={{0,8},{8,0},{16,24},{24,16},{1,9},{9,1},{17,25},{25,17},{2,10},{10... | collective-permute-start | bytes 73736 | tf_op jit(solution)/shard_map/ppermute | solution.py:644
  18.2 33.5 %collective-permute-start.5 = (f32[8,768]{1,0:T(8,128)S(1)}, f32[8,768]{1,0:T(8,128)S(1)}, u32[]{:S(2)}, u32[]{:S(2)}) collective-permute-start(f32[8,768]{1,0:T(8,128)S(1)} %concatenate.28), channel_id=1, source_target_pairs={{0,16},{8,24},{16,0},{24,8},{1,17},{9,25},{17,1},{25,9},{2,18},{10... | collective-permute-start | bytes 73736 | tf_op jit(solution)/shard_map/ppermute | solution.py:644
  20.2 31.5 %collective-permute-start.6 = (f32[8,768]{1,0:T(8,128)S(1)}, f32[8,768]{1,0:T(8,128)S(1)}, u32[]{:S(2)}, u32[]{:S(2)}) collective-permute-start(f32[8,768]{1,0:T(8,128)S(1)} %concatenate.28), channel_id=1, source_target_pairs={{0,24},{8,16},{16,8},{24,0},{1,25},{9,17},{17,9},{25,1},{2,26},{10... | collective-permute-start | bytes 73736 | tf_op jit(solution)/shard_map/ppermute | solution.py:644
  51.7 39.0 %copy-start.1 = (bf16[400,3072]{1,0:T(8,128)(2,1)}, bf16[400,3072]{1,0:T(8,128)(2,1)S(1)}, u32[]{:S(2)}) copy-start(bf16[400,3072]{1,0:T(8,128)(2,1)S(1)} %collective-permute-done.refs_10_.refs_8_) | copy-start | bytes 7372804
  51.7 30.3 %collective-permute-start.8 = (bf16[400,3072]{1,0:T(8,128)(2,1)S(1)}, bf16[400,3072]{1,0:T(8,128)(2,1)}, u32[]{:S(2)}, u32[]{:S(2)}) collective-permute-start(bf16[400,3072]{1,0:T(8,128)(2,1)S(1)} %collective-permute-done.refs_10_.refs_8_), channel_id=1, source_target_pairs={{0,8},{1,17},{8,0},{9,25},{16,24},{17,1},{24,16},{25,9},{2,10},{3,... | collective-permute-start | bytes 7372808 | tf_op jit(solution)/shard_map/ppermute | solution.py:651
  54.0 28.8 %collective-permute-start.7 = (bf16[208,3072]{1,0:T(8,128)(2,1)}, bf16[208,3072]{1,0:T(8,128)(2,1)}, u32[]{:S(2)}, u32[]{:S(2)}) collective-permute-start(bf16[208,3072]{1,0:T(8,128)(2,1)} %collective-permute-done.1.refs_8_.refs_6_), channel_id=1, source_target_pairs={{0,2},{2,0},{4,6},{6,4},{1,3},{3,1},{5,7},{7,5},{8,10},{10,8},{12,... | collective-permute-start | bytes 3833864 | tf_op jit(solution)/shard_map/ppermute | solution.py:680
  55.6 33.3 %collective-permute-start.11 = (bf16[400,3072]{1,0:T(8,128)(2,1)S(1)}, bf16[400,3072]{1,0:T(8,128)(2,1)}, u32[]{:S(2)}, u32[]{:S(2)}) collective-permute-start(bf16[400,3072]{1,0:T(8,128)(2,1)S(1)} %collective-permute-done.refs_10_.refs_8_), channel_id=1, source_target_pairs={{0,1},{1,0},{2,3},{3,2},{4,5},{5,4},{6,7},{7,6},{8,9},{9,8},{10,11... | collective-permute-start | bytes 7372808 | tf_op jit(solution)/shard_map/ppermute | solution.py:647
  82.0 8.7 %collective-permute-start.12 = (bf16[400,3072]{1,0:T(8,128)(2,1)}, bf16[400,3072]{1,0:T(8,128)(2,1)}, u32[]{:S(2)}, u32[]{:S(2)}) collective-permute-start(bf16[400,3072]{1,0:T(8,128)(2,1)} %collective-permute-done.8.refs_11_.refs_9_), channel_id=1, source_target_pairs={{0,1},{1,0},{2,3},{3,2},{4,5},{5,4},{6,7},{7,6},{8,9},{9,8},{10,11... | collective-permute-start | bytes 7372808 | tf_op jit(solution)/shard_map/ppermute | solution.py:647
  82.0 6.8 %collective-permute-start.9 = (bf16[208,3072]{1,0:T(8,128)(2,1)}, bf16[208,3072]{1,0:T(8,128)(2,1)}, u32[]{:S(2)}, u32[]{:S(2)}) collective-permute-start(bf16[208,3072]{1,0:T(8,128)(2,1)} %collective-permute-done.1.refs_8_.refs_6_), channel_id=1, source_target_pairs={{0,1},{1,0},{2,3},{3,2},{4,5},{5,4},{6,7},{7,6},{8,9},{9,8},{10,11... | collective-permute-start | bytes 3833864 | tf_op jit(solution)/shard_map/ppermute | solution.py:647
  82.8 7.9 %collective-permute-start.10 = (bf16[208,3072]{1,0:T(8,128)(2,1)}, bf16[208,3072]{1,0:T(8,128)(2,1)}, u32[]{:S(2)}, u32[]{:S(2)}) collective-permute-start(bf16[208,3072]{1,0:T(8,128)(2,1)} %collective-permute-done.7.refs_9_.refs_7_), channel_id=1, source_target_pairs={{0,1},{1,0},{2,3},{3,2},{4,5},{5,4},{6,7},{7,6},{8,9},{9,8},{10,11... | collective-permute-start | bytes 3833864 | tf_op jit(solution)/shard_map/ppermute | solution.py:647
  83.6 7.1 %copy-start.4 = (s32[512]{0:T(512)}, s32[512]{0:T(512)S(1)}, u32[]{:S(2)}) copy-start(s32[512]{0:T(512)S(1)} %pad_add_fusion.1) | copy-start | bytes 6148
  138.0 47.0 %all-to-all-start = ((bf16[8,256,768]{2,1,0:T(8,128)(2,1)}), bf16[8,256,768]{2,1,0:T(8,128)(2,1)S(1)}, u32[]{:S(2)}, u32[]{:S(2)}) async-start(bf16[8,256,768]{2,1,0:T(8,128)(2,1)} %get-tuple-element.53), calls=%async_computation | async-start | bytes 6291456 | tf_op jit(solution)/shard_map/all_to_all | solution.py:703
  185.0 15.4 %copy-start = (bf16[8,256,768]{2,1,0:T(8,128)(2,1)}, bf16[8,256,768]{2,1,0:T(8,128)(2,1)S(1)}, u32[]{:S(2)}) copy-start(bf16[8,256,768]{2,1,0:T(8,128)(2,1)S(1)} %all-to-all-done.refs_0_) | copy-start | bytes 9437188
  185.0 19.8 %copy-start.3 = (bf16[160,768]{1,0:T(8,128)(2,1)S(1)}, bf16[160,768]{1,0:T(8,128)(2,1)}, u32[]{:S(2)}) copy-start(bf16[160,768]{1,0:T(8,128)(2,1)} %get-tuple-element.80) | copy-start | bytes 737284
  185.0 9.1 %collective-permute-start.13 = (bf16[160,768]{1,0:T(8,128)(2,1)}, bf16[160,768]{1,0:T(8,128)(2,1)}, u32[]{:S(2)}, u32[]{:S(2)}) collective-permute-start(bf16[160,768]{1,0:T(8,128)(2,1)} %get-tuple-element.75), channel_id=1, source_target_pairs={{0,8},{8,0},{16,24},{24,16},{1,9},{9,1},{17,25},{25,17},{2,10},{10... | collective-permute-start | bytes 737288 | tf_op jit(solution)/shard_map/ppermute | solution.py:644
  187.1 13.3 %collective-permute-start.14 = (bf16[160,768]{1,0:T(8,128)(2,1)}, bf16[160,768]{1,0:T(8,128)(2,1)}, u32[]{:S(2)}, u32[]{:S(2)}) collective-permute-start(bf16[160,768]{1,0:T(8,128)(2,1)} %get-tuple-element.76), channel_id=1, source_target_pairs={{0,16},{8,24},{16,0},{24,8},{1,17},{9,25},{17,1},{25,9},{2,18},{10... | collective-permute-start | bytes 737288 | tf_op jit(solution)/shard_map/ppermute | solution.py:644
  188.6 11.8 %collective-permute-start.15 = (bf16[160,768]{1,0:T(8,128)(2,1)}, bf16[160,768]{1,0:T(8,128)(2,1)}, u32[]{:S(2)}, u32[]{:S(2)}) collective-permute-start(bf16[160,768]{1,0:T(8,128)(2,1)} %get-tuple-element.77), channel_id=1, source_target_pairs={{0,24},{8,16},{16,8},{24,0},{1,25},{9,17},{17,9},{25,1},{2,26},{10... | collective-permute-start | bytes 737288 | tf_op jit(solution)/shard_map/ppermute | solution.py:644
  200.4 42.4 %all-to-all-start.1 = ((bf16[8,256,768]{2,1,0:T(8,128)(2,1)}), bf16[8,256,768]{2,1,0:T(8,128)(2,1)}, u32[]{:S(2)}, u32[]{:S(2)}) async-start(bf16[8,256,768]{2,1,0:T(8,128)(2,1)} %get-tuple-element.79), calls=%async_computation.1 | async-start | bytes 6291456 | tf_op jit(solution)/shard_map/all_to_all | solution.py:703
  206.1 1.6 collective-permute-start.16
  207.8 8.3 %collective-permute-start.17 = (bf16[160,768]{1,0:T(8,128)(2,1)S(1)}, bf16[160,768]{1,0:T(8,128)(2,1)S(1)}, u32[]{:S(2)}, u32[]{:S(2)}) collective-permute-start(bf16[160,768]{1,0:T(8,128)(2,1)S(1)} %add_convert_fusion.2), channel_id=1, source_target_pairs={{0,2},{2,0},{4,6},{6,4},{1,3},{3,1},{5,7},{7,5},{8,10},{10,8},{12,... | collective-permute-start | bytes 737288 | tf_op jit(solution)/shard_map/ppermute | solution.py:721
  216.1 13.7 %collective-permute-start.18 = (bf16[160,768]{1,0:T(8,128)(2,1)S(1)}, bf16[160,768]{1,0:T(8,128)(2,1)S(1)}, u32[]{:S(2)}, u32[]{:S(2)}) collective-permute-start(bf16[160,768]{1,0:T(8,128)(2,1)S(1)} %add_convert_fusion.1), channel_id=1, source_target_pairs={{0,4},{2,6},{4,0},{6,2},{1,5},{3,7},{5,1},{7,3},{8,12},{10,14},{12... | collective-permute-start | bytes 737288 | tf_op jit(solution)/shard_map/ppermute | solution.py:721
where the time goes:
time: 247 us; the launch traced here: 246 us
  waiting for transfers between devices  96.7 us (39%)
  Pallas kernels  92.7 us (38%)
  starting transfers between devices  30 us (12%)
  local copies, waits for them, and re-layouts  14.9 us (6%)
  other arithmetic  11.2 us (5%)
    pallas_call x3, Pallas kernels, run(): pl.pallas_call(wrapped, out_shape=[shape for shape, _ in outs], in_specs=...  92.7 us
    ppermute x6, waiting for transfers between devices, sect(): return lax.ppermute(x, 'section', [(i, i ^ apart) for i in sections])  38.4 us
    ppermute x3, waiting for transfers between devices, by_core(): return lax.ppermute(x, ('section', 'core'), pairs)  26.4 us
    ppermute x2, waiting for transfers between devices, per_device(): lax.ppermute(total, 'group', [(i, i ^ apart) for i in range(n_group)])  15 us
    all_to_all x2, waiting for transfers between devices, to_owners(): return lax.all_to_all(x, ('section', 'core'), 0, 0, tiled=True)  10.9 us
    all_to_all x2, starting transfers between devices, to_owners(): return lax.all_to_all(x, ('section', 'core'), 0, 0, tiled=True)  8.74 us
    ppermute x6, starting transfers between devices, sect(): return lax.ppermute(x, 'section', [(i, i ^ apart) for i in sections])  7.17 us
    ppermute x3, starting transfers between devices, by_core(): return lax.ppermute(x, ('section', 'core'), pairs)  6.78 us
  transfers between devices with their start and end apart: 21, of which 12 were waited for; matrix products, arithmetic and copies ran while one was open for 7% of the time, Pallas kernels for 18%

commit v1 on v0

--- a/solution.py
+++ b/solution.py
@@ -9,6 +9,7 @@
 GROUP = 2
 PARTS = 4
 EXTRA = 32
+SUMS = 16
 COST = 1e8
 BF = jnp.bfloat16
 F32 = jnp.float32
@@ -83,7 +84,7 @@
         return self.ref.at[pl.ds(self.used - count, count)]
 
 
-def load_slab(sems, src, block, weights, slab_v):
+def load_slab(sems, src, block, weights, slab_v, order=range(PARTS)):
     own, own_pack, bufs = weights
     rows = own.shape[0] // GROUP
     plane = src[block, GROUP + 2]
@@ -93,7 +94,7 @@
 
             @pl.when(src[block, h] == i)
             def _():
-                for p in range(PARTS):
+                for p in order:
                     columns = pl.ds(p * (own.shape[1] // PARTS), own.shape[1] // PARTS)
                     for n, buf in enumerate(parts):
                         first = h * rows if i == 0 else 0
@@ -112,10 +113,9 @@
     pltpu.make_async_copy(own.at[:, columns], slab_v.at[:, columns], sems.at[p]).wait()
 
 
-def load_down(sems, down, layer, down_v):
-    for p in range(PARTS):
-        rows = pl.ds(p * (down_v.shape[0] // PARTS), down_v.shape[0] // PARTS)
-        pltpu.make_async_copy(down.at[layer, rows], down_v.at[rows], sems.at[p]).start()
+def load_down(sems, down, layer, down_v, p):
+    rows = pl.ds(p * (down_v.shape[0] // PARTS), down_v.shape[0] // PARTS)
+    pltpu.make_async_copy(down.at[layer, rows], down_v.at[rows], sems.at[p]).start()
 
 
 def down_part(sems, down, down_v, p):
@@ -229,7 +229,7 @@
         [jnp.sum(v, axis=0, keepdims=True) for v in (s_upb, s_gain, s_bias)]
         + [jnp.concatenate([jnp.sum(s_downb, axis=0, keepdims=True),
                             jnp.zeros((1, width - 128), F32)], axis=1),
-           jnp.zeros((EXTRA - 4, width), F32)], axis=0)
+           jnp.zeros((SUMS - 4, width), F32)], axis=0)
     grads_ref[2 * adapt :, :] = tail.astype(BF)
 
     def body2(i, carry):
@@ -440,8 +440,9 @@
             qkv, ctx, probs = buf_a[:3]
             project(y_v.at[1], slab, qkv, lambda i: slab_part(slab_sems[0], wts, slab, i))
             slab_part(slab_sems[0], wts, slab, PARTS - 1)
-            load_slab(slab_sems[1], src_ref, b + 1, wts, slabs.at[1])
-            load_down(down_sems, down_ref, layer, down_v)
+            for p in range(PARTS):
+                load_slab(slab_sems[1], src_ref, b + 1, wts, slabs.at[1], [p])
+                load_down(down_sems, down_ref, layer, down_v, p)
             attend(qkv, bias_v, probs, ctx)
             by_columns(acc, lambda cols: dot(
                 ctx[...], slab[:, 3 * width + cols.start : 3 * width + cols.stop]))
@@ -512,23 +513,28 @@
         buf_a, buf_f = scratch[12 : 12 + n_a], scratch[12 + n_a :]
         sems = Sems(sem_ref)
         slab_sems = [sems.run(PARTS) for i in range(2)]
-        down_sems, pack_sems = sems.run(PARTS), sems.run(2)
-        group_a, group_f, group_dy = Group(sems, n_a), Group(sems, n_f), Group(sems, 1)
+        down_sems, slope_sems, pack_sems = sems.run(PARTS), sems.run(PARTS), sems.run(2)
+        group_a, post_a = Group(sems, 3), Group(sems, n_a - 3)
+        post_f, group_dy = Group(sems, n_f - 1), Group(sems, 1)
         rows_sems, grads_sems = sems.run(2), sems.run(2)
         core = src_ref[0, GROUP + 1]
 
-        def load_a(layer):
-            return [(x.at[layer], buf) for x, buf in zip(in_a[3:] + in_a[:3], buf_a[3:] + buf_a[:3])]
-
-        def load_f(layer):
-            return [(x.at[layer], buf) for x, buf in zip(in_f[1:] + in_f[:1], buf_f[1:] + buf_f[:1])]
+        def pairs(refs, bufs, layer):
+            return [(x.at[layer], buf) for x, buf in zip(refs, bufs)]
+
+        def slope_part(layer, p):
+            columns = part_of(ff, p)
+            return pltpu.make_async_copy(in_f[0].at[layer, :, columns], buf_f[0].at[:, columns],
+                                         slope_sems.at[p])
 
         def fetch_f(layer):
             b = 2 * layer + 1
-            group_f.start(*load_f(layer))
+            post_f.start(*pairs(in_f[1:], buf_f[1:], layer))
             load_pack(pack_sems.at[0], src_ref, b, wts, packs.at[0])
-            load_down(down_sems, down_ref, layer, down_v)
-            load_slab(slab_sems[0], src_ref, b, wts, slabs.at[0])
+            for p in range(PARTS):
+                load_down(down_sems, down_ref, layer, down_v, p)
+                slope_part(layer, p).start()
+                load_slab(slab_sems[0], src_ref, b, wts, slabs.at[0], [p])
 
         def wait_pack(i):
             pltpu.make_async_copy(wts[1], packs.at[i], pack_sems.at[i]).wait()
@@ -550,18 +556,21 @@
             def _():
                 wait_sent(0, dx_v)
 
-            group_f.wait(*load_f(0))
+            post_f.wait(*pairs(in_f[1:], buf_f[1:], 0))
             wait_pack(0)
             post_backward(packs.at[0], small_ref.at[src_ref[b, GROUP]], dy_v, buf_f[1:], acc, db,
                           grads.at[0], dpt, adapt)
             send_grads(grads_sems.at[0], grads.at[0], src_ref[b, GROUP], grads_out)
             load_pack(pack_sems.at[1], src_ref, b - 1, wts, packs.at[1])
-            group_a.start(*load_a(layer))
-            load_slab(slab_sems[1], src_ref, b - 1, wts, slabs.at[1])
+            post_a.start(*pairs(in_a[3:], buf_a[3:], layer))
+            load_slab(slab_sems[1], src_ref, b - 1, wts, slabs.at[1], [PARTS - 1])
+            group_a.start(*pairs(in_a[:3], buf_a[:3], layer))
+            load_slab(slab_sems[1], src_ref, b - 1, wts, slabs.at[1], range(PARTS - 1))
 
             def ready(i):
                 slab_part(slab_sems[0], wts, slabs.at[0], i)
                 down_part(down_sems, down_ref, down_v, i)
+                slope_part(0, i).wait()
 
             ffn_branch_back(db, slabs.at[0], down_v, buf_f[0], acc, ready)
             dx_v[...] = acc[...].astype(BF)
@@ -572,7 +581,7 @@
             def _():
                 wait_sent(1, dy_v)
 
-            group_a.wait(*load_a(0))
+            post_a.wait(*pairs(in_a[3:], buf_a[3:], 0))
             wait_pack(1)
 
             @pl.when(layer > 0)
@@ -583,10 +592,12 @@
                           db, grads.at[1], dpt, adapt)
             send_grads(grads_sems.at[1], grads.at[1], src_ref[b - 1, GROUP], grads_out)
             slab = slabs.at[1]
-            for i in range(PARTS):
+            slab_part(slab_sems[1], wts, slab, PARTS - 1)
+            by_columns(dc_v, lambda cols: dot_t(db[...], slab[cols, 3 * width :]))
+            group_a.wait(*pairs(in_a[:3], buf_a[:3], 0))
+            attend_back(buf_a[0], buf_a[1], dc_v, buf_a[2], dqkv)
+            for i in range(PARTS - 1):
                 slab_part(slab_sems[1], wts, slab, i)
-            by_columns(dc_v, lambda cols: dot_t(db[...], slab[cols, 3 * width :]))
-            attend_back(buf_a[0], buf_a[1], dc_v, buf_a[2], dqkv)
             by_columns(dy_v, lambda cols: acc[:, cols] + dot_t(dqkv[...], slab[cols, : 3 * width]))
             for copy in row_copies(dy_v, b - 1, core, sent, rows_sems.at[1]):
                 copy.start()
@@ -596,7 +607,7 @@
         wait_sent(0, dx_v)
         wait_sent(1, dy_v)
 
-    grad_shape = (2 * adapt + EXTRA, width)
+    grad_shape = (2 * adapt + SUMS, width)
     outs = [(like((2 * layers * GROUP, rows // GROUP, width)), ANY)]
     outs += [(like(grad_shape), ANY)] * (2 * layers)
     scratch = [
@@ -714,7 +725,7 @@
     for part in coming:
         total = total + part.astype(F32)
     total = total.astype(BF)
-    input_grads = to_owners(leaving)
+    input_grads = settle(to_owners(leaving))
     total = (total.astype(F32) + peer(total).astype(F32)).astype(BF)
     apart = 1
     while apart < n_group:

time: 247 us -> 245 us (level)
  local copies, waits for them, and re-layouts: 14.9 us -> 11.1 us
  Pallas kernels: 92.7 us -> 95.2 us
    unnamed x19 -> x18, local copies, waits for them, and re-layouts: 3.81 us -> 0.05 us
    pallas_call x3 -> x4, Pallas kernels: 92.7 us -> 95.2 us  [run(): pl.pallas_call(wrapped, out_shape=[shape for shape, _ in outs], in_specs=...]
  transfers between devices with their start and end apart: 21 -> 21, of which waited for: 12 -> 12; matrix products, arithmetic and copies ran while one was open for 7% -> 7% of each run, Pallas kernels for 18% -> 19%
where the time goes in v1:
time: 245 us; the launch traced here: 244 us
  waiting for transfers between devices  95.7 us (39%)
  Pallas kernels  95.2 us (39%)
  starting transfers between devices  30.1 us (12%)
  other arithmetic  11.1 us (5%)
  local copies, waits for them, and re-layouts  11.1 us (5%)
    pallas_call x4, Pallas kernels, run(): pl.pallas_call(wrapped, out_shape=[shape for shape, _ in outs], in_specs=...  95.2 us
    ppermute x6, waiting for transfers between devices, sect(): return lax.ppermute(x, 'section', [(i, i ^ apart) for i in sections])  37.4 us
    ppermute x3, waiting for transfers between devices, by_core(): return lax.ppermute(x, ('section', 'core'), pairs)  26.4 us
    ppermute x2, waiting for transfers between devices, per_device(): lax.ppermute(total, 'group', [(i, i ^ apart) for i in range(n_group)])  13.4 us
    all_to_all x2, waiting for transfers between devices, to_owners(): return lax.all_to_all(x, ('section', 'core'), 0, 0, tiled=True)  12.6 us
    all_to_all x2, starting transfers between devices, to_owners(): return lax.all_to_all(x, ('section', 'core'), 0, 0, tiled=True)  8.73 us
    ppermute x6, starting transfers between devices, sect(): return lax.ppermute(x, 'section', [(i, i ^ apart) for i in sections])  7.19 us
    ppermute x3, starting transfers between devices, by_core(): return lax.ppermute(x, ('section', 'core'), pairs)  6.78 us
  transfers between devices with their start and end apart: 21, of which 12 were waited for; matrix products, arithmetic and copies ran while one was open for 7% of the time, Pallas kernels for 19%

profile of v1, /device:TPU:0, one launch (start us, length us, event | category | flops | bytes accessed | tf_op | source)
XLA Modules:
  0.0 244.4 jit_solution(14496772980165077458)
XLA Ops:
  0.6 0.9 convert.10
  1.6 0.9 convert_bitcast_fusion
  2.6 0.0 copy-start.2
  2.6 1.9 dynamic-slice_bitcast_fusion
  4.5 1.6 pad_maximum_fusion
  6.1 3.0 %collective-permute-start = (bf16[400,3072]{1,0:T(8,128)(2,1)}, bf16[400,3072]{1,0:T(8,128)(2,1)S(1)}, u32[]{:S(2)}, u32[]{:S(2)}) collective-permute-start(bf16[400,3072]{1,0:T(8,128)(2,1)} %pad_maximum_fusion), channel_id=1, source_target_pairs={{0,16},{1,9},{8,24},{9,1},{16,0},{17,25},{24,8},{25,17},{2,18},{3,... | collective-permute-start | bytes 7372808 | tf_op jit(solution)/shard_map/ppermute | solution.py:662
  9.1 1.3 dynamic-slice_bitcast_fusion.1
  10.4 0.0 copy-start.8
  10.4 0.0 copy-start.5
  10.4 0.0 copy-start.6
  10.5 0.0 copy-start.7
  10.5 1.1 pad_maximum_fusion.1
  11.6 1.5 collective-permute-start.1
  13.1 2.0 dynamic-slice_bitcast_fusion.5
  15.1 1.9 dynamic-slice_bitcast_fusion.3
  17.0 0.5 collective-permute-start.3
  17.6 0.6 collective-permute-start.4
  18.2 0.1 collective-permute-start.5
  18.2 1.9 pad_maximum_fusion.2.refs_1_
  20.2 2.9 %collective-permute-start.6 = (f32[8,768]{1,0:T(8,128)S(1)}, f32[8,768]{1,0:T(8,128)S(1)}, u32[]{:S(2)}, u32[]{:S(2)}) collective-permute-start(f32[8,768]{1,0:T(8,128)S(1)} %concatenate.28), channel_id=1, source_target_pairs={{0,24},{8,16},{16,8},{24,0},{1,25},{9,17},{17,9},{25,1},{2,26},{10... | collective-permute-start | bytes 73736 | tf_op jit(solution)/shard_map/ppermute | solution.py:655
  23.1 1.9 pad_maximum_fusion.3.refs_1_
  25.0 18.4 %collective-permute-done.4 = f32[8,768]{1,0:T(8,128)S(1)} collective-permute-done((f32[8,768]{1,0:T(8,128)S(1)}, f32[8,768]{1,0:T(8,128)S(1)}, u32[]{:S(2)}, u32[]{:S(2)}) %collective-permute-start.4) | collective-permute-done | bytes 24608 | tf_op jit(solution)/shard_map/ppermute | solution.py:655
  43.4 8.3 %collective-permute-done.5 = f32[8,768]{1,0:T(8,128)S(1)} collective-permute-done((f32[8,768]{1,0:T(8,128)S(1)}, f32[8,768]{1,0:T(8,128)S(1)}, u32[]{:S(2)}, u32[]{:S(2)}) %collective-permute-start.5) | collective-permute-done | bytes 24608 | tf_op jit(solution)/shard_map/ppermute | solution.py:655
  51.7 0.0 copy-start.1
  51.7 2.3 collective-permute-start.8
  54.0 1.6 collective-permute-start.7
  55.6 26.4 %collective-permute-done.8.refs_11_.refs_9_ = bf16[400,3072]{1,0:T(8,128)(2,1)} collective-permute-done((bf16[400,3072]{1,0:T(8,128)(2,1)S(1)}, bf16[400,3072]{1,0:T(8,128)(2,1)}, u32[]{:S(2)}, u32[]{:S(2)}) %collective-permute-start.8) | collective-permute-done | bytes 2457632 | tf_op jit(solution)/shard_map/ppermute | solution.py:662
  82.0 0.5 collective-permute-start.9
  82.5 0.3 collective-permute-done.7.refs_9_.refs_7_
  82.8 0.8 fusion.3
  83.6 0.9 copy.19.refs_2_
  84.5 0.1 stack.110
  84.6 0.1 stack.105
  84.6 0.1 stack.100
  84.7 0.1 stack.95
  84.8 0.6 pad_add_fusion.refs_0_
  85.4 0.6 pad_maximum_fusion.5.refs_4_.refs_2_
  86.1 2.8 %collective-permute-done.9.refs_12_.refs_10_ = bf16[208,3072]{1,0:T(8,128)(2,1)} collective-permute-done((bf16[208,3072]{1,0:T(8,128)(2,1)}, bf16[208,3072]{1,0:T(8,128)(2,1)}, u32[]{:S(2)}, u32[]{:S(2)}) %collective-permute-start.9) | collective-permute-done | bytes 1277984 | tf_op jit(solution)/shard_map/ppermute | solution.py:658
  88.8 1.8 collective-permute-done.10.refs_13_.refs_11_
  90.7 47.3 %forward.1 = (bf16[2,512,2304]{2,1,0:T(8,128)(2,1)}, bf16[2,512,768]{2,1,0:T(8,128)(2,1)}, bf16[2,12,512,512]{3,2,1,0:T(8,128)(2,1)}, bf16[2,512,768]{2,1,0:T(8,...) custom-call(s32[4,5]{1,0:T(4,128)} %pad_add_fusion.refs_0_, ...), custom_call_target="tpu_custom_call" | custom-call | flops 6000000000 | tf_op jit(solution)/shard_map/forward/pallas_call | solution.py:52
  137.9 4.3 %all-to-all-start = ((bf16[8,256,768]{2,1,0:T(8,128)(2,1)}), bf16[8,256,768]{2,1,0:T(8,128)(2,1)S(1)}, u32[]{:S(2)}, u32[]{:S(2)}) async-start(bf16[8,256,768]{2,1,0:T(8,128)(2,1)} %get-tuple-element.53), calls=%async_computation | async-start | bytes 6291456 | tf_op jit(solution)/shard_map/all_to_all | solution.py:714
  142.2 42.5 %backward.1 = (bf16[8,256,768]{2,1,0:T(8,128)(2,1)}, bf16[144,768]{1,0:T(8,128)(2,1)}, bf16[144,768]{1,0:T(8,128)(2,1)}, bf16[144,768]{1,0:T(8,128)(2,1)}, bf16[144,768]{1,0:T(8,128)(2,1)}) custom-call(s32[4,5]{1,0:T(4,128)} %pad_add_fusion.refs_0_, bf16[512,768]{1,0:T(8,128)(2,1)} %pad_maximum_fusion.3.refs_1_, ...), custom_call_target="tpu_custom_call" | custom-call | flops 6000000000 | tf_op jit(solution)/shard_map/backward/pallas_call | solution.py:52
  184.8 0.0 copy-start
  184.8 2.1 collective-permute-start.13
  186.9 1.5 collective-permute-start.14
  188.3 0.1 collective-permute-start.15
  188.4 5.0 %collective-permute-done.13 = bf16[144,768]{1,0:T(8,128)(2,1)} collective-permute-done((bf16[144,768]{1,0:T(8,128)(2,1)}, bf16[144,768]{1,0:T(8,128)(2,1)}, u32[]{:S(2)}, u32[]{:S(2)}) %collective-permute-start.13) | collective-permute-done | bytes 221216 | tf_op jit(solution)/shard_map/ppermute | solution.py:655
  193.4 5.7 %collective-permute-done.14 = bf16[144,768]{1,0:T(8,128)(2,1)} collective-permute-done((bf16[144,768]{1,0:T(8,128)(2,1)}, bf16[144,768]{1,0:T(8,128)(2,1)}, u32[]{:S(2)}, u32[]{:S(2)}) %collective-permute-start.14) | collective-permute-done | bytes 221216 | tf_op jit(solution)/shard_map/ppermute | solution.py:655
  199.1 4.5 %all-to-all-start.1 = ((bf16[8,256,768]{2,1,0:T(8,128)(2,1)}), bf16[8,256,768]{2,1,0:T(8,128)(2,1)}, u32[]{:S(2)}, u32[]{:S(2)}) async-start(bf16[8,256,768]{2,1,0:T(8,128)(2,1)} %get-tuple-element.79), calls=%async_computation.1 | async-start | bytes 6291456 | tf_op jit(solution)/shard_map/all_to_all | solution.py:714
  203.6 1.3 add_convert_fusion.3
  204.9 0.4 collective-permute-start.16
  205.3 1.1 collective-permute-done.16
  206.4 0.1 add_convert_fusion.2
  206.5 1.7 collective-permute-start.17
  208.2 6.1 %collective-permute-done.17 = bf16[144,768]{1,0:T(8,128)(2,1)S(1)} collective-permute-done((bf16[144,768]{1,0:T(8,128)(2,1)S(1)}, bf16[144,768]{1,0:T(8,128)(2,1)S(1)}, u32[]{:S(2)}, u32[]{:S(2)}) %collective-permute-start.17) | collective-permute-done | bytes 221216 | tf_op jit(solution)/shard_map/ppermute | solution.py:732
  214.2 0.1 add_convert_fusion.1
  214.3 2.7 %collective-permute-start.18 = (bf16[144,768]{1,0:T(8,128)(2,1)S(1)}, bf16[144,768]{1,0:T(8,128)(2,1)S(1)}, u32[]{:S(2)}, u32[]{:S(2)}) collective-permute-start(bf16[144,768]{1,0:T(8,128)(2,1)S(1)} %add_convert_fusion.1), channel_id=1, source_target_pairs={{0,4},{2,6},{4,0},{6,2},{1,5},{3,7},{5,1},{7,3},{8,12},{10,14},{12... | collective-permute-start | bytes 663560 | tf_op jit(solution)/shard_map/ppermute | solution.py:732
  217.0 2.7 %settle.2 = bf16[8,256,768]{2,1,0:T(8,128)(2,1)} custom-call(bf16[8,256,768]{2,1,0:T(8,128)(2,1)} %copy-done), custom_call_target="tpu_custom_call" | custom-call | flops 300000000 | tf_op jit(solution)/shard_map/settle/pallas_call | solution.py:52
  219.7 7.3 %collective-permute-done.18 = bf16[144,768]{1,0:T(8,128)(2,1)S(1)} collective-permute-done((bf16[144,768]{1,0:T(8,128)(2,1)S(1)}, bf16[144,768]{1,0:T(8,128)(2,1)S(1)}, u32[]{:S(2)}, u32[]{:S(2)}) %collective-permute-start.18) | collective-permute-done | bytes 221216 | tf_op jit(solution)/shard_map/ppermute | solution.py:732
  227.1 0.5 slice.57
  227.6 0.6 fusion.1
  228.2 0.8 slice_bitcast_fusion
  228.9 12.6 %all-to-all-done.1.refs_0_ = bf16[8,256,768]{2,1,0:T(8,128)(2,1)} async-done(((bf16[8,256,768]{2,1,0:T(8,128)(2,1)}), bf16[8,256,768]{2,1,0:T(8,128)(2,1)}, u32[]{:S(2)}, u32[]{:S(2)}) %all-to-all-start.1) | async-done | bytes 3145760 | tf_op jit(solution)/shard_map/all_to_all | solution.py:714
  241.5 2.7 %settle.3 = bf16[8,256,768]{2,1,0:T(8,128)(2,1)} custom-call(bf16[8,256,768]{2,1,0:T(8,128)(2,1)} %all-to-all-done.1.refs_0_), custom_call_target="tpu_custom_call" | custom-call | flops 300000000 | tf_op jit(solution)/shard_map/settle/pallas_call | solution.py:52
  (33 shorter events, 0.2 us)
Async XLA Ops:
  2.6 1.9 copy-start.2
  6.1 45.5 %collective-permute-start = (bf16[400,3072]{1,0:T(8,128)(2,1)}, bf16[400,3072]{1,0:T(8,128)(2,1)S(1)}, u32[]{:S(2)}, u32[]{:S(2)}) collective-permute-start(bf16[400,3072]{1,0:T(8,128)(2,1)} %pad_maximum_fusion), channel_id=1, source_target_pairs={{0,16},{1,9},{8,24},{9,1},{16,0},{17,25},{24,8},{25,17},{2,18},{3,... | collective-permute-start | bytes 7372808 | tf_op jit(solution)/shard_map/ppermute | solution.py:662
  10.4 7.1 %copy-start.8 = (f32[1,64]{1,0:T(1,128)S(1)}, f32[1,64]{1,0:T(1,128)}, u32[]{:S(2)}) copy-start(f32[1,64]{1,0:T(1,128)} %param.17) | copy-start | bytes 772
  10.4 7.1 %copy-start.5 = (f32[1,768]{1,0:T(1,128)S(1)}, f32[1,768]{1,0:T(1,128)}, u32[]{:S(2)}) copy-start(f32[1,768]{1,0:T(1,128)} %param.19) | copy-start | bytes 9220
  10.4 7.1 %copy-start.6 = (f32[1,768]{1,0:T(1,128)S(1)}, f32[1,768]{1,0:T(1,128)}, u32[]{:S(2)}) copy-start(f32[1,768]{1,0:T(1,128)} %param.20) | copy-start | bytes 9220
  10.5 7.1 %copy-start.7 = (f32[1,768]{1,0:T(1,128)S(1)}, f32[1,768]{1,0:T(1,128)}, u32[]{:S(2)}) copy-start(f32[1,768]{1,0:T(1,128)} %param.21) | copy-start | bytes 9220
  11.6 40.0 %collective-permute-start.1 = (bf16[208,3072]{1,0:T(8,128)(2,1)}, bf16[208,3072]{1,0:T(8,128)(2,1)}, u32[]{:S(2)}, u32[]{:S(2)}) collective-permute-start(bf16[208,3072]{1,0:T(8,128)(2,1)} %pad_maximum_fusion.1), channel_id=1, source_target_pairs={{0,8},{1,17},{8,0},{9,25},{16,24},{17,1},{24,16},{25,9},{2,10},{3,... | collective-permute-start | bytes 3833864 | tf_op jit(solution)/shard_map/ppermute | solution.py:662
  15.1 3.1 %collective-permute-start.2 = (bf16[256,768]{1,0:T(8,128)(2,1)}, bf16[256,768]{1,0:T(8,128)(2,1)}, u32[]{:S(2)}, u32[]{:S(2)}) collective-permute-start(bf16[256,768]{1,0:T(8,128)(2,1)} %get-tuple-element.87), channel_id=1, source_target_pairs={{0,1},{1,0},{2,3},{3,2},{4,5},{5,4},{6,7},{7,6},{8,9},{9,8},{10,11... | collective-permute-start | bytes 1179656 | tf_op jit(solution)/shard_map/ppermute | solution.py:658
  17.0 3.2 %collective-permute-start.3 = (bf16[256,768]{1,0:T(8,128)(2,1)}, bf16[256,768]{1,0:T(8,128)(2,1)}, u32[]{:S(2)}, u32[]{:S(2)}) collective-permute-start(bf16[256,768]{1,0:T(8,128)(2,1)} %get-tuple-element.85), channel_id=1, source_target_pairs={{0,1},{1,0},{2,3},{3,2},{4,5},{5,4},{6,7},{7,6},{8,9},{9,8},{10,11... | collective-permute-start | bytes 1179656 | tf_op jit(solution)/shard_map/ppermute | solution.py:658
  17.6 25.8 %collective-permute-start.4 = (f32[8,768]{1,0:T(8,128)S(1)}, f32[8,768]{1,0:T(8,128)S(1)}, u32[]{:S(2)}, u32[]{:S(2)}) collective-permute-start(f32[8,768]{1,0:T(8,128)S(1)} %concatenate.28), channel_id=1, source_target_pairs={{0,8},{8,0},{16,24},{24,16},{1,9},{9,1},{17,25},{25,17},{2,10},{10... | collective-permute-start | bytes 73736 | tf_op jit(solution)/shard_map/ppermute | solution.py:655
  18.2 33.5 %collective-permute-start.5 = (f32[8,768]{1,0:T(8,128)S(1)}, f32[8,768]{1,0:T(8,128)S(1)}, u32[]{:S(2)}, u32[]{:S(2)}) collective-permute-start(f32[8,768]{1,0:T(8,128)S(1)} %concatenate.28), channel_id=1, source_target_pairs={{0,16},{8,24},{16,0},{24,8},{1,17},{9,25},{17,1},{25,9},{2,18},{10... | collective-permute-start | bytes 73736 | tf_op jit(solution)/shard_map/ppermute | solution.py:655
  20.2 31.5 %collective-permute-start.6 = (f32[8,768]{1,0:T(8,128)S(1)}, f32[8,768]{1,0:T(8,128)S(1)}, u32[]{:S(2)}, u32[]{:S(2)}) collective-permute-start(f32[8,768]{1,0:T(8,128)S(1)} %concatenate.28), channel_id=1, source_target_pairs={{0,24},{8,16},{16,8},{24,0},{1,25},{9,17},{17,9},{25,1},{2,26},{10... | collective-permute-start | bytes 73736 | tf_op jit(solution)/shard_map/ppermute | solution.py:655
  51.7 39.0 %copy-start.1 = (bf16[400,3072]{1,0:T(8,128)(2,1)}, bf16[400,3072]{1,0:T(8,128)(2,1)S(1)}, u32[]{:S(2)}) copy-start(bf16[400,3072]{1,0:T(8,128)(2,1)S(1)} %collective-permute-done.refs_10_.refs_8_) | copy-start | bytes 7372804
  51.7 30.3 %collective-permute-start.8 = (bf16[400,3072]{1,0:T(8,128)(2,1)S(1)}, bf16[400,3072]{1,0:T(8,128)(2,1)}, u32[]{:S(2)}, u32[]{:S(2)}) collective-permute-start(bf16[400,3072]{1,0:T(8,128)(2,1)S(1)} %collective-permute-done.refs_10_.refs_8_), channel_id=1, source_target_pairs={{0,8},{1,17},{8,0},{9,25},{16,24},{17,1},{24,16},{25,9},{2,10},{3,... | collective-permute-start | bytes 7372808 | tf_op jit(solution)/shard_map/ppermute | solution.py:662
  54.0 28.8 %collective-permute-start.7 = (bf16[208,3072]{1,0:T(8,128)(2,1)}, bf16[208,3072]{1,0:T(8,128)(2,1)}, u32[]{:S(2)}, u32[]{:S(2)}) collective-permute-start(bf16[208,3072]{1,0:T(8,128)(2,1)} %collective-permute-done.1.refs_8_.refs_6_), channel_id=1, source_target_pairs={{0,2},{2,0},{4,6},{6,4},{1,3},{3,1},{5,7},{7,5},{8,10},{10,8},{12,... | collective-permute-start | bytes 3833864 | tf_op jit(solution)/shard_map/ppermute | solution.py:691
  55.6 33.3 %collective-permute-start.11 = (bf16[400,3072]{1,0:T(8,128)(2,1)S(1)}, bf16[400,3072]{1,0:T(8,128)(2,1)}, u32[]{:S(2)}, u32[]{:S(2)}) collective-permute-start(bf16[400,3072]{1,0:T(8,128)(2,1)S(1)} %collective-permute-done.refs_10_.refs_8_), channel_id=1, source_target_pairs={{0,1},{1,0},{2,3},{3,2},{4,5},{5,4},{6,7},{7,6},{8,9},{9,8},{10,11... | collective-permute-start | bytes 7372808 | tf_op jit(solution)/shard_map/ppermute | solution.py:658
  82.0 8.7 %collective-permute-start.12 = (bf16[400,3072]{1,0:T(8,128)(2,1)}, bf16[400,3072]{1,0:T(8,128)(2,1)}, u32[]{:S(2)}, u32[]{:S(2)}) collective-permute-start(bf16[400,3072]{1,0:T(8,128)(2,1)} %collective-permute-done.8.refs_11_.refs_9_), channel_id=1, source_target_pairs={{0,1},{1,0},{2,3},{3,2},{4,5},{5,4},{6,7},{7,6},{8,9},{9,8},{10,11... | collective-permute-start | bytes 7372808 | tf_op jit(solution)/shard_map/ppermute | solution.py:658
  82.0 6.8 %collective-permute-start.9 = (bf16[208,3072]{1,0:T(8,128)(2,1)}, bf16[208,3072]{1,0:T(8,128)(2,1)}, u32[]{:S(2)}, u32[]{:S(2)}) collective-permute-start(bf16[208,3072]{1,0:T(8,128)(2,1)} %collective-permute-done.1.refs_8_.refs_6_), channel_id=1, source_target_pairs={{0,1},{1,0},{2,3},{3,2},{4,5},{5,4},{6,7},{7,6},{8,9},{9,8},{10,11... | collective-permute-start | bytes 3833864 | tf_op jit(solution)/shard_map/ppermute | solution.py:658
  82.8 7.9 %collective-permute-start.10 = (bf16[208,3072]{1,0:T(8,128)(2,1)}, bf16[208,3072]{1,0:T(8,128)(2,1)}, u32[]{:S(2)}, u32[]{:S(2)}) collective-permute-start(bf16[208,3072]{1,0:T(8,128)(2,1)} %collective-permute-done.7.refs_9_.refs_7_), channel_id=1, source_target_pairs={{0,1},{1,0},{2,3},{3,2},{4,5},{5,4},{6,7},{7,6},{8,9},{9,8},{10,11... | collective-permute-start | bytes 3833864 | tf_op jit(solution)/shard_map/ppermute | solution.py:658
  83.6 7.1 %copy-start.4 = (s32[512]{0:T(512)}, s32[512]{0:T(512)S(1)}, u32[]{:S(2)}) copy-start(s32[512]{0:T(512)S(1)} %pad_add_fusion.1) | copy-start | bytes 6148
  137.9 46.8 %all-to-all-start = ((bf16[8,256,768]{2,1,0:T(8,128)(2,1)}), bf16[8,256,768]{2,1,0:T(8,128)(2,1)S(1)}, u32[]{:S(2)}, u32[]{:S(2)}) async-start(bf16[8,256,768]{2,1,0:T(8,128)(2,1)} %get-tuple-element.53), calls=%async_computation | async-start | bytes 6291456 | tf_op jit(solution)/shard_map/all_to_all | solution.py:714
  184.8 14.4 %copy-start = (bf16[8,256,768]{2,1,0:T(8,128)(2,1)}, bf16[8,256,768]{2,1,0:T(8,128)(2,1)S(1)}, u32[]{:S(2)}) copy-start(bf16[8,256,768]{2,1,0:T(8,128)(2,1)S(1)} %all-to-all-done.refs_0_) | copy-start | bytes 9437188
  184.8 18.8 %copy-start.3 = (bf16[144,768]{1,0:T(8,128)(2,1)S(1)}, bf16[144,768]{1,0:T(8,128)(2,1)}, u32[]{:S(2)}) copy-start(bf16[144,768]{1,0:T(8,128)(2,1)} %get-tuple-element.80) | copy-start | bytes 663556
  184.8 8.6 %collective-permute-start.13 = (bf16[144,768]{1,0:T(8,128)(2,1)}, bf16[144,768]{1,0:T(8,128)(2,1)}, u32[]{:S(2)}, u32[]{:S(2)}) collective-permute-start(bf16[144,768]{1,0:T(8,128)(2,1)} %get-tuple-element.75), channel_id=1, source_target_pairs={{0,8},{8,0},{16,24},{24,16},{1,9},{9,1},{17,25},{25,17},{2,10},{10... | collective-permute-start | bytes 663560 | tf_op jit(solution)/shard_map/ppermute | solution.py:655
  186.9 12.3 %collective-permute-start.14 = (bf16[144,768]{1,0:T(8,128)(2,1)}, bf16[144,768]{1,0:T(8,128)(2,1)}, u32[]{:S(2)}, u32[]{:S(2)}) collective-permute-start(bf16[144,768]{1,0:T(8,128)(2,1)} %get-tuple-element.76), channel_id=1, source_target_pairs={{0,16},{8,24},{16,0},{24,8},{1,17},{9,25},{17,1},{25,9},{2,18},{10... | collective-permute-start | bytes 663560 | tf_op jit(solution)/shard_map/ppermute | solution.py:655
  188.3 10.8 %collective-permute-start.15 = (bf16[144,768]{1,0:T(8,128)(2,1)}, bf16[144,768]{1,0:T(8,128)(2,1)}, u32[]{:S(2)}, u32[]{:S(2)}) collective-permute-start(bf16[144,768]{1,0:T(8,128)(2,1)} %get-tuple-element.77), channel_id=1, source_target_pairs={{0,24},{8,16},{16,8},{24,0},{1,25},{9,17},{17,9},{25,1},{2,26},{10... | collective-permute-start | bytes 663560 | tf_op jit(solution)/shard_map/ppermute | solution.py:655
  199.1 42.4 %all-to-all-start.1 = ((bf16[8,256,768]{2,1,0:T(8,128)(2,1)}), bf16[8,256,768]{2,1,0:T(8,128)(2,1)}, u32[]{:S(2)}, u32[]{:S(2)}) async-start(bf16[8,256,768]{2,1,0:T(8,128)(2,1)} %get-tuple-element.79), calls=%async_computation.1 | async-start | bytes 6291456 | tf_op jit(solution)/shard_map/all_to_all | solution.py:714
  204.9 1.5 collective-permute-start.16
  206.5 7.8 %collective-permute-start.17 = (bf16[144,768]{1,0:T(8,128)(2,1)S(1)}, bf16[144,768]{1,0:T(8,128)(2,1)S(1)}, u32[]{:S(2)}, u32[]{:S(2)}) collective-permute-start(bf16[144,768]{1,0:T(8,128)(2,1)S(1)} %add_convert_fusion.2), channel_id=1, source_target_pairs={{0,2},{2,0},{4,6},{6,4},{1,3},{3,1},{5,7},{7,5},{8,10},{10,8},{12,... | collective-permute-start | bytes 663560 | tf_op jit(solution)/shard_map/ppermute | solution.py:732
  214.3 12.7 %collective-permute-start.18 = (bf16[144,768]{1,0:T(8,128)(2,1)S(1)}, bf16[144,768]{1,0:T(8,128)(2,1)S(1)}, u32[]{:S(2)}, u32[]{:S(2)}) collective-permute-start(bf16[144,768]{1,0:T(8,128)(2,1)S(1)} %add_convert_fusion.1), channel_id=1, source_target_pairs={{0,4},{2,6},{4,0},{6,2},{1,5},{3,7},{5,1},{7,3},{8,12},{10,14},{12... | collective-permute-start | bytes 663560 | tf_op jit(solution)/shard_map/ppermute | solution.py:732

commit v2 on v1

--- a/solution.py
+++ b/solution.py
@@ -250,23 +250,22 @@
 
 
 def ffn_branch(x_ref, slab, down, slope_ref, acc, ready, step=256):
-    acc[...] = jnp.zeros_like(acc)
     size = slab.shape[1] // PARTS
-
-    def part(i, carry):
-        ready(i)
-        act, before = None, None
-        for j in range(size // step):
-            cols = pl.ds(pl.multiple_of(i * size + j * step, step), step)
-            values, slope = gelu_pair(dot(x_ref[...], slab[:, cols]))
-            slope_ref[:, cols] = slope.astype(BF)
-            if act is not None:
-                acc[...] += dot(act, down[before, :])
-            act, before = values.astype(BF), cols
-        acc[...] += dot(act, down[before, :])
-        return carry
-
-    lax.fori_loop(0, PARTS, part, 0, unroll=2)
+    before = None
+    for i in range(PARTS + 1):
+        if i < PARTS:
+            ready(i)
+            acts = []
+            for j in range(size // step):
+                cols = slice(i * size + j * step, i * size + (j + 1) * step)
+                values, slope = gelu_pair(dot(x_ref[...], slab[:, cols]))
+                slope_ref[:, cols] = slope.astype(BF)
+                acts.append(values.astype(BF))
+        if i == 1:
+            acc[...] = dot(before, down[:size, :])
+        elif i > 1:
+            acc[...] += dot(before, down[(i - 1) * size : i * size, :])
+        before = jnp.concatenate(acts, axis=1)
 
 
 def ffn_branch_back(db, slab, down, slope_ref, acc, ready, step=256):
@@ -406,7 +405,8 @@
         sems = Sems(sem_ref)
         slab_sems = [sems.run(PARTS) for b in range(2)]
         down_sems, pack_sem = sems.run(PARTS), sems.run(1).at[0]
-        group_a, group_f = Group(sems, n_a), Group(sems, len(buf_f))
+        group_a, group_f = Group(sems, n_a), Group(sems, len(buf_f) - 1)
+        group_slope = Group(sems, 1)
         rows_sems = sems.run(2)
         core = src_ref[0, GROUP + 1]
 
@@ -459,7 +459,8 @@
 
             @pl.when(layer > 0)
             def _():
-                group_f.wait(*save_f(0))
+                group_slope.wait(save_f(0)[0])
+                group_f.wait(*save_f(0)[1:])
                 wait_rows(1)
 
             def ready(i):
@@ -467,16 +468,18 @@
                 down_part(down_sems, down_ref, down_v, i)
 
             ffn_branch(y_v.at[0], slabs.at[1], down_v, buf_f[0], acc, ready)
+            group_slope.start(save_f(layer)[0])
             post_forward(packs.at[b + 1], small_ref.at[src_ref[b + 1, GROUP]], y_v.at[0], acc,
                          y_v.at[1], buf_f[1:], adapt)
             for copy in row_copies(y_v.at[1], b + 1, core, sent, rows_sems.at[1]):
                 copy.start()
-            group_f.start(*save_f(layer))
+            group_f.start(*save_f(layer)[1:])
             return carry
 
         lax.fori_loop(0, layers, layer_step, 0)
         group_a.wait(*save_a(0))
-        group_f.wait(*save_f(0))
+        group_slope.wait(save_f(0)[0])
+        group_f.wait(*save_f(0)[1:])
         for i in range(2):
             wait_rows(i)
 

time: 245 us -> 244 us (level)
  no operation moved by 1% of the time
where the time goes in v2:
time: 244 us; the launch traced here: 243 us
  waiting for transfers between devices  95.8 us (39%)
  Pallas kernels  93.7 us (38%)
  starting transfers between devices  30.1 us (12%)
  other arithmetic  11.1 us (5%)
  local copies, waits for them, and re-layouts  11.1 us (5%)
    pallas_call x4, Pallas kernels, run(): pl.pallas_call(wrapped, out_shape=[shape for shape, _ in outs], in_specs=...  93.7 us
    ppermute x6, waiting for transfers between devices, sect(): return lax.ppermute(x, 'section', [(i, i ^ apart) for i in sections])  37.4 us
    ppermute x3, waiting for transfers between devices, by_core(): return lax.ppermute(x, ('section', 'core'), pairs)  26.4 us
    ppermute x2, waiting for transfers between devices, per_device(): lax.ppermute(total, 'group', [(i, i ^ apart) for i in range(n_group)])  13.4 us
    all_to_all x2, waiting for transfers between devices, to_owners(): return lax.all_to_all(x, ('section', 'core'), 0, 0, tiled=True)  12.6 us
    all_to_all x2, starting transfers between devices, to_owners(): return lax.all_to_all(x, ('section', 'core'), 0, 0, tiled=True)  8.73 us
    ppermute x6, starting transfers between devices, sect(): return lax.ppermute(x, 'section', [(i, i ^ apart) for i in sections])  7.2 us
    ppermute x3, starting transfers between devices, by_core(): return lax.ppermute(x, ('section', 'core'), pairs)  6.78 us
  transfers between devices with their start and end apart: 21, of which 12 were waited for; matrix products, arithmetic and copies ran while one was open for 7% of the time, Pallas kernels for 19%

profile of v2, /device:TPU:0, one launch (start us, length us, event | category | flops | bytes accessed | tf_op | source)
XLA Modules:
  0.0 242.8 jit_solution(16169417111656802456)
XLA Ops:
  0.6 0.9 convert.10
  1.6 0.9 convert_bitcast_fusion
  2.6 0.0 copy-start.2
  2.6 1.9 dynamic-slice_bitcast_fusion
  4.5 1.6 pad_maximum_fusion
  6.1 3.0 %collective-permute-start = (bf16[400,3072]{1,0:T(8,128)(2,1)}, bf16[400,3072]{1,0:T(8,128)(2,1)S(1)}, u32[]{:S(2)}, u32[]{:S(2)}) collective-permute-start(bf16[400,3072]{1,0:T(8,128)(2,1)} %pad_maximum_fusion), channel_id=1, source_target_pairs={{0,16},{1,9},{8,24},{9,1},{16,0},{17,25},{24,8},{25,17},{2,18},{3,... | collective-permute-start | bytes 7372808 | tf_op jit(solution)/shard_map/ppermute | solution.py:665
  9.1 1.3 dynamic-slice_bitcast_fusion.1
  10.4 0.0 copy-start.8
  10.4 0.0 copy-start.5
  10.4 0.0 copy-start.6
  10.5 0.0 copy-start.7
  10.5 1.1 pad_maximum_fusion.1
  11.6 1.5 collective-permute-start.1
  13.1 2.0 dynamic-slice_bitcast_fusion.5
  15.1 1.9 dynamic-slice_bitcast_fusion.3
  17.0 0.5 collective-permute-start.3
  17.6 0.6 collective-permute-start.4
  18.2 0.1 collective-permute-start.5
  18.2 1.9 pad_maximum_fusion.2.refs_1_
  20.2 2.9 %collective-permute-start.6 = (f32[8,768]{1,0:T(8,128)S(1)}, f32[8,768]{1,0:T(8,128)S(1)}, u32[]{:S(2)}, u32[]{:S(2)}) collective-permute-start(f32[8,768]{1,0:T(8,128)S(1)} %concatenate.28), channel_id=1, source_target_pairs={{0,24},{8,16},{16,8},{24,0},{1,25},{9,17},{17,9},{25,1},{2,26},{10... | collective-permute-start | bytes 73736 | tf_op jit(solution)/shard_map/ppermute | solution.py:658
  23.1 1.9 pad_maximum_fusion.3.refs_1_
  25.0 18.4 %collective-permute-done.4 = f32[8,768]{1,0:T(8,128)S(1)} collective-permute-done((f32[8,768]{1,0:T(8,128)S(1)}, f32[8,768]{1,0:T(8,128)S(1)}, u32[]{:S(2)}, u32[]{:S(2)}) %collective-permute-start.4) | collective-permute-done | bytes 24608 | tf_op jit(solution)/shard_map/ppermute | solution.py:658
  43.4 8.3 %collective-permute-done.5 = f32[8,768]{1,0:T(8,128)S(1)} collective-permute-done((f32[8,768]{1,0:T(8,128)S(1)}, f32[8,768]{1,0:T(8,128)S(1)}, u32[]{:S(2)}, u32[]{:S(2)}) %collective-permute-start.5) | collective-permute-done | bytes 24608 | tf_op jit(solution)/shard_map/ppermute | solution.py:658
  51.7 0.0 copy-start.1
  51.7 2.3 collective-permute-start.8
  54.0 1.6 collective-permute-start.7
  55.6 26.4 %collective-permute-done.8.refs_11_.refs_9_ = bf16[400,3072]{1,0:T(8,128)(2,1)} collective-permute-done((bf16[400,3072]{1,0:T(8,128)(2,1)S(1)}, bf16[400,3072]{1,0:T(8,128)(2,1)}, u32[]{:S(2)}, u32[]{:S(2)}) %collective-permute-start.8) | collective-permute-done | bytes 2457632 | tf_op jit(solution)/shard_map/ppermute | solution.py:665
  82.0 0.5 collective-permute-start.9
  82.5 0.3 collective-permute-done.7.refs_9_.refs_7_
  82.8 0.8 fusion.3
  83.6 0.9 copy.19.refs_2_
  84.5 0.1 stack.110
  84.6 0.1 stack.105
  84.6 0.1 stack.100
  84.7 0.1 stack.95
  84.8 0.6 pad_add_fusion.refs_0_
  85.4 0.6 pad_maximum_fusion.5.refs_4_.refs_2_
  86.1 2.8 %collective-permute-done.9.refs_12_.refs_10_ = bf16[208,3072]{1,0:T(8,128)(2,1)} collective-permute-done((bf16[208,3072]{1,0:T(8,128)(2,1)}, bf16[208,3072]{1,0:T(8,128)(2,1)}, u32[]{:S(2)}, u32[]{:S(2)}) %collective-permute-start.9) | collective-permute-done | bytes 1277984 | tf_op jit(solution)/shard_map/ppermute | solution.py:661
  88.8 1.8 collective-permute-done.10.refs_13_.refs_11_
  90.7 45.7 %forward.1 = (bf16[2,512,2304]{2,1,0:T(8,128)(2,1)}, bf16[2,512,768]{2,1,0:T(8,128)(2,1)}, bf16[2,12,512,512]{3,2,1,0:T(8,128)(2,1)}, bf16[2,512,768]{2,1,0:T(8,...) custom-call(s32[4,5]{1,0:T(4,128)} %pad_add_fusion.refs_0_, ...), custom_call_target="tpu_custom_call" | custom-call | flops 6000000000 | tf_op jit(solution)/shard_map/forward/pallas_call | solution.py:52
  136.4 4.3 %all-to-all-start = ((bf16[8,256,768]{2,1,0:T(8,128)(2,1)}), bf16[8,256,768]{2,1,0:T(8,128)(2,1)S(1)}, u32[]{:S(2)}, u32[]{:S(2)}) async-start(bf16[8,256,768]{2,1,0:T(8,128)(2,1)} %get-tuple-element.53), calls=%async_computation | async-start | bytes 6291456 | tf_op jit(solution)/shard_map/all_to_all | solution.py:717
  140.7 42.5 %backward.1 = (bf16[8,256,768]{2,1,0:T(8,128)(2,1)}, bf16[144,768]{1,0:T(8,128)(2,1)}, bf16[144,768]{1,0:T(8,128)(2,1)}, bf16[144,768]{1,0:T(8,128)(2,1)}, bf16[144,768]{1,0:T(8,128)(2,1)}) custom-call(s32[4,5]{1,0:T(4,128)} %pad_add_fusion.refs_0_, bf16[512,768]{1,0:T(8,128)(2,1)} %pad_maximum_fusion.3.refs_1_, ...), custom_call_target="tpu_custom_call" | custom-call | flops 6000000000 | tf_op jit(solution)/shard_map/backward/pallas_call | solution.py:52
  183.2 0.0 copy-start
  183.2 2.1 collective-permute-start.13
  185.3 1.5 collective-permute-start.14
  186.8 0.1 collective-permute-start.15
  186.9 5.0 %collective-permute-done.13 = bf16[144,768]{1,0:T(8,128)(2,1)} collective-permute-done((bf16[144,768]{1,0:T(8,128)(2,1)}, bf16[144,768]{1,0:T(8,128)(2,1)}, u32[]{:S(2)}, u32[]{:S(2)}) %collective-permute-start.13) | collective-permute-done | bytes 221216 | tf_op jit(solution)/shard_map/ppermute | solution.py:658
  191.8 5.7 %collective-permute-done.14 = bf16[144,768]{1,0:T(8,128)(2,1)} collective-permute-done((bf16[144,768]{1,0:T(8,128)(2,1)}, bf16[144,768]{1,0:T(8,128)(2,1)}, u32[]{:S(2)}, u32[]{:S(2)}) %collective-permute-start.14) | collective-permute-done | bytes 221216 | tf_op jit(solution)/shard_map/ppermute | solution.py:658
  197.6 4.5 %all-to-all-start.1 = ((bf16[8,256,768]{2,1,0:T(8,128)(2,1)}), bf16[8,256,768]{2,1,0:T(8,128)(2,1)}, u32[]{:S(2)}, u32[]{:S(2)}) async-start(bf16[8,256,768]{2,1,0:T(8,128)(2,1)} %get-tuple-element.79), calls=%async_computation.1 | async-start | bytes 6291456 | tf_op jit(solution)/shard_map/all_to_all | solution.py:717
  202.1 1.3 add_convert_fusion.3
  203.3 0.4 collective-permute-start.16
  203.8 1.1 collective-permute-done.16
  204.9 0.1 add_convert_fusion.2
  204.9 1.7 collective-permute-start.17
  206.6 6.1 %collective-permute-done.17 = bf16[144,768]{1,0:T(8,128)(2,1)S(1)} collective-permute-done((bf16[144,768]{1,0:T(8,128)(2,1)S(1)}, bf16[144,768]{1,0:T(8,128)(2,1)S(1)}, u32[]{:S(2)}, u32[]{:S(2)}) %collective-permute-start.17) | collective-permute-done | bytes 221216 | tf_op jit(solution)/shard_map/ppermute | solution.py:735
  212.7 0.1 add_convert_fusion.1
  212.8 2.6 %collective-permute-start.18 = (bf16[144,768]{1,0:T(8,128)(2,1)S(1)}, bf16[144,768]{1,0:T(8,128)(2,1)S(1)}, u32[]{:S(2)}, u32[]{:S(2)}) collective-permute-start(bf16[144,768]{1,0:T(8,128)(2,1)S(1)} %add_convert_fusion.1), channel_id=1, source_target_pairs={{0,4},{2,6},{4,0},{6,2},{1,5},{3,7},{5,1},{7,3},{8,12},{10,14},{12... | collective-permute-start | bytes 663560 | tf_op jit(solution)/shard_map/ppermute | solution.py:735
  215.4 2.7 %settle.2 = bf16[8,256,768]{2,1,0:T(8,128)(2,1)} custom-call(bf16[8,256,768]{2,1,0:T(8,128)(2,1)} %copy-done), custom_call_target="tpu_custom_call" | custom-call | flops 300000000 | tf_op jit(solution)/shard_map/settle/pallas_call | solution.py:52
  218.1 7.3 %collective-permute-done.18 = bf16[144,768]{1,0:T(8,128)(2,1)S(1)} collective-permute-done((bf16[144,768]{1,0:T(8,128)(2,1)S(1)}, bf16[144,768]{1,0:T(8,128)(2,1)S(1)}, u32[]{:S(2)}, u32[]{:S(2)}) %collective-permute-start.18) | collective-permute-done | bytes 221216 | tf_op jit(solution)/shard_map/ppermute | solution.py:735
  225.5 0.5 slice.57
  226.0 0.6 fusion.1
  226.6 0.8 slice_bitcast_fusion
  227.4 12.6 %all-to-all-done.1.refs_0_ = bf16[8,256,768]{2,1,0:T(8,128)(2,1)} async-done(((bf16[8,256,768]{2,1,0:T(8,128)(2,1)}), bf16[8,256,768]{2,1,0:T(8,128)(2,1)}, u32[]{:S(2)}, u32[]{:S(2)}) %all-to-all-start.1) | async-done | bytes 3145760 | tf_op jit(solution)/shard_map/all_to_all | solution.py:717
  239.9 2.7 %settle.3 = bf16[8,256,768]{2,1,0:T(8,128)(2,1)} custom-call(bf16[8,256,768]{2,1,0:T(8,128)(2,1)} %all-to-all-done.1.refs_0_), custom_call_target="tpu_custom_call" | custom-call | flops 300000000 | tf_op jit(solution)/shard_map/settle/pallas_call | solution.py:52
  (33 shorter events, 0.2 us)
Async XLA Ops:
  2.6 1.9 copy-start.2
  6.1 45.5 %collective-permute-start = (bf16[400,3072]{1,0:T(8,128)(2,1)}, bf16[400,3072]{1,0:T(8,128)(2,1)S(1)}, u32[]{:S(2)}, u32[]{:S(2)}) collective-permute-start(bf16[400,3072]{1,0:T(8,128)(2,1)} %pad_maximum_fusion), channel_id=1, source_target_pairs={{0,16},{1,9},{8,24},{9,1},{16,0},{17,25},{24,8},{25,17},{2,18},{3,... | collective-permute-start | bytes 7372808 | tf_op jit(solution)/shard_map/ppermute | solution.py:665
  10.4 7.1 %copy-start.8 = (f32[1,64]{1,0:T(1,128)S(1)}, f32[1,64]{1,0:T(1,128)}, u32[]{:S(2)}) copy-start(f32[1,64]{1,0:T(1,128)} %param.17) | copy-start | bytes 772
  10.4 7.1 %copy-start.5 = (f32[1,768]{1,0:T(1,128)S(1)}, f32[1,768]{1,0:T(1,128)}, u32[]{:S(2)}) copy-start(f32[1,768]{1,0:T(1,128)} %param.19) | copy-start | bytes 9220
  10.4 7.1 %copy-start.6 = (f32[1,768]{1,0:T(1,128)S(1)}, f32[1,768]{1,0:T(1,128)}, u32[]{:S(2)}) copy-start(f32[1,768]{1,0:T(1,128)} %param.20) | copy-start | bytes 9220
  10.5 7.1 %copy-start.7 = (f32[1,768]{1,0:T(1,128)S(1)}, f32[1,768]{1,0:T(1,128)}, u32[]{:S(2)}) copy-start(f32[1,768]{1,0:T(1,128)} %param.21) | copy-start | bytes 9220
  11.6 40.0 %collective-permute-start.1 = (bf16[208,3072]{1,0:T(8,128)(2,1)}, bf16[208,3072]{1,0:T(8,128)(2,1)}, u32[]{:S(2)}, u32[]{:S(2)}) collective-permute-start(bf16[208,3072]{1,0:T(8,128)(2,1)} %pad_maximum_fusion.1), channel_id=1, source_target_pairs={{0,8},{1,17},{8,0},{9,25},{16,24},{17,1},{24,16},{25,9},{2,10},{3,... | collective-permute-start | bytes 3833864 | tf_op jit(solution)/shard_map/ppermute | solution.py:665
  15.1 3.1 %collective-permute-start.2 = (bf16[256,768]{1,0:T(8,128)(2,1)}, bf16[256,768]{1,0:T(8,128)(2,1)}, u32[]{:S(2)}, u32[]{:S(2)}) collective-permute-start(bf16[256,768]{1,0:T(8,128)(2,1)} %get-tuple-element.87), channel_id=1, source_target_pairs={{0,1},{1,0},{2,3},{3,2},{4,5},{5,4},{6,7},{7,6},{8,9},{9,8},{10,11... | collective-permute-start | bytes 1179656 | tf_op jit(solution)/shard_map/ppermute | solution.py:661
  17.0 3.2 %collective-permute-start.3 = (bf16[256,768]{1,0:T(8,128)(2,1)}, bf16[256,768]{1,0:T(8,128)(2,1)}, u32[]{:S(2)}, u32[]{:S(2)}) collective-permute-start(bf16[256,768]{1,0:T(8,128)(2,1)} %get-tuple-element.85), channel_id=1, source_target_pairs={{0,1},{1,0},{2,3},{3,2},{4,5},{5,4},{6,7},{7,6},{8,9},{9,8},{10,11... | collective-permute-start | bytes 1179656 | tf_op jit(solution)/shard_map/ppermute | solution.py:661
  17.6 25.8 %collective-permute-start.4 = (f32[8,768]{1,0:T(8,128)S(1)}, f32[8,768]{1,0:T(8,128)S(1)}, u32[]{:S(2)}, u32[]{:S(2)}) collective-permute-start(f32[8,768]{1,0:T(8,128)S(1)} %concatenate.28), channel_id=1, source_target_pairs={{0,8},{8,0},{16,24},{24,16},{1,9},{9,1},{17,25},{25,17},{2,10},{10... | collective-permute-start | bytes 73736 | tf_op jit(solution)/shard_map/ppermute | solution.py:658
  18.2 33.5 %collective-permute-start.5 = (f32[8,768]{1,0:T(8,128)S(1)}, f32[8,768]{1,0:T(8,128)S(1)}, u32[]{:S(2)}, u32[]{:S(2)}) collective-permute-start(f32[8,768]{1,0:T(8,128)S(1)} %concatenate.28), channel_id=1, source_target_pairs={{0,16},{8,24},{16,0},{24,8},{1,17},{9,25},{17,1},{25,9},{2,18},{10... | collective-permute-start | bytes 73736 | tf_op jit(solution)/shard_map/ppermute | solution.py:658
  20.2 31.5 %collective-permute-start.6 = (f32[8,768]{1,0:T(8,128)S(1)}, f32[8,768]{1,0:T(8,128)S(1)}, u32[]{:S(2)}, u32[]{:S(2)}) collective-permute-start(f32[8,768]{1,0:T(8,128)S(1)} %concatenate.28), channel_id=1, source_target_pairs={{0,24},{8,16},{16,8},{24,0},{1,25},{9,17},{17,9},{25,1},{2,26},{10... | collective-permute-start | bytes 73736 | tf_op jit(solution)/shard_map/ppermute | solution.py:658
  51.7 39.0 %copy-start.1 = (bf16[400,3072]{1,0:T(8,128)(2,1)}, bf16[400,3072]{1,0:T(8,128)(2,1)S(1)}, u32[]{:S(2)}) copy-start(bf16[400,3072]{1,0:T(8,128)(2,1)S(1)} %collective-permute-done.refs_10_.refs_8_) | copy-start | bytes 7372804
  51.7 30.3 %collective-permute-start.8 = (bf16[400,3072]{1,0:T(8,128)(2,1)S(1)}, bf16[400,3072]{1,0:T(8,128)(2,1)}, u32[]{:S(2)}, u32[]{:S(2)}) collective-permute-start(bf16[400,3072]{1,0:T(8,128)(2,1)S(1)} %collective-permute-done.refs_10_.refs_8_), channel_id=1, source_target_pairs={{0,8},{1,17},{8,0},{9,25},{16,24},{17,1},{24,16},{25,9},{2,10},{3,... | collective-permute-start | bytes 7372808 | tf_op jit(solution)/shard_map/ppermute | solution.py:665
  54.0 28.8 %collective-permute-start.7 = (bf16[208,3072]{1,0:T(8,128)(2,1)}, bf16[208,3072]{1,0:T(8,128)(2,1)}, u32[]{:S(2)}, u32[]{:S(2)}) collective-permute-start(bf16[208,3072]{1,0:T(8,128)(2,1)} %collective-permute-done.1.refs_8_.refs_6_), channel_id=1, source_target_pairs={{0,2},{2,0},{4,6},{6,4},{1,3},{3,1},{5,7},{7,5},{8,10},{10,8},{12,... | collective-permute-start | bytes 3833864 | tf_op jit(solution)/shard_map/ppermute | solution.py:694
  55.6 33.3 %collective-permute-start.11 = (bf16[400,3072]{1,0:T(8,128)(2,1)S(1)}, bf16[400,3072]{1,0:T(8,128)(2,1)}, u32[]{:S(2)}, u32[]{:S(2)}) collective-permute-start(bf16[400,3072]{1,0:T(8,128)(2,1)S(1)} %collective-permute-done.refs_10_.refs_8_), channel_id=1, source_target_pairs={{0,1},{1,0},{2,3},{3,2},{4,5},{5,4},{6,7},{7,6},{8,9},{9,8},{10,11... | collective-permute-start | bytes 7372808 | tf_op jit(solution)/shard_map/ppermute | solution.py:661
  82.0 8.7 %collective-permute-start.12 = (bf16[400,3072]{1,0:T(8,128)(2,1)}, bf16[400,3072]{1,0:T(8,128)(2,1)}, u32[]{:S(2)}, u32[]{:S(2)}) collective-permute-start(bf16[400,3072]{1,0:T(8,128)(2,1)} %collective-permute-done.8.refs_11_.refs_9_), channel_id=1, source_target_pairs={{0,1},{1,0},{2,3},{3,2},{4,5},{5,4},{6,7},{7,6},{8,9},{9,8},{10,11... | collective-permute-start | bytes 7372808 | tf_op jit(solution)/shard_map/ppermute | solution.py:661
  82.0 6.8 %collective-permute-start.9 = (bf16[208,3072]{1,0:T(8,128)(2,1)}, bf16[208,3072]{1,0:T(8,128)(2,1)}, u32[]{:S(2)}, u32[]{:S(2)}) collective-permute-start(bf16[208,3072]{1,0:T(8,128)(2,1)} %collective-permute-done.1.refs_8_.refs_6_), channel_id=1, source_target_pairs={{0,1},{1,0},{2,3},{3,2},{4,5},{5,4},{6,7},{7,6},{8,9},{9,8},{10,11... | collective-permute-start | bytes 3833864 | tf_op jit(solution)/shard_map/ppermute | solution.py:661
  82.8 7.9 %collective-permute-start.10 = (bf16[208,3072]{1,0:T(8,128)(2,1)}, bf16[208,3072]{1,0:T(8,128)(2,1)}, u32[]{:S(2)}, u32[]{:S(2)}) collective-permute-start(bf16[208,3072]{1,0:T(8,128)(2,1)} %collective-permute-done.7.refs_9_.refs_7_), channel_id=1, source_target_pairs={{0,1},{1,0},{2,3},{3,2},{4,5},{5,4},{6,7},{7,6},{8,9},{9,8},{10,11... | collective-permute-start | bytes 3833864 | tf_op jit(solution)/shard_map/ppermute | solution.py:661
  83.6 7.1 %copy-start.4 = (s32[512]{0:T(512)}, s32[512]{0:T(512)S(1)}, u32[]{:S(2)}) copy-start(s32[512]{0:T(512)S(1)} %pad_add_fusion.1) | copy-start | bytes 6148
  136.4 46.8 %all-to-all-start = ((bf16[8,256,768]{2,1,0:T(8,128)(2,1)}), bf16[8,256,768]{2,1,0:T(8,128)(2,1)S(1)}, u32[]{:S(2)}, u32[]{:S(2)}) async-start(bf16[8,256,768]{2,1,0:T(8,128)(2,1)} %get-tuple-element.53), calls=%async_computation | async-start | bytes 6291456 | tf_op jit(solution)/shard_map/all_to_all | solution.py:717
  183.2 14.4 %copy-start = (bf16[8,256,768]{2,1,0:T(8,128)(2,1)}, bf16[8,256,768]{2,1,0:T(8,128)(2,1)S(1)}, u32[]{:S(2)}) copy-start(bf16[8,256,768]{2,1,0:T(8,128)(2,1)S(1)} %all-to-all-done.refs_0_) | copy-start | bytes 9437188
  183.2 18.8 %copy-start.3 = (bf16[144,768]{1,0:T(8,128)(2,1)S(1)}, bf16[144,768]{1,0:T(8,128)(2,1)}, u32[]{:S(2)}) copy-start(bf16[144,768]{1,0:T(8,128)(2,1)} %get-tuple-element.80) | copy-start | bytes 663556
  183.2 8.6 %collective-permute-start.13 = (bf16[144,768]{1,0:T(8,128)(2,1)}, bf16[144,768]{1,0:T(8,128)(2,1)}, u32[]{:S(2)}, u32[]{:S(2)}) collective-permute-start(bf16[144,768]{1,0:T(8,128)(2,1)} %get-tuple-element.75), channel_id=1, source_target_pairs={{0,8},{8,0},{16,24},{24,16},{1,9},{9,1},{17,25},{25,17},{2,10},{10... | collective-permute-start | bytes 663560 | tf_op jit(solution)/shard_map/ppermute | solution.py:658
  185.3 12.3 %collective-permute-start.14 = (bf16[144,768]{1,0:T(8,128)(2,1)}, bf16[144,768]{1,0:T(8,128)(2,1)}, u32[]{:S(2)}, u32[]{:S(2)}) collective-permute-start(bf16[144,768]{1,0:T(8,128)(2,1)} %get-tuple-element.76), channel_id=1, source_target_pairs={{0,16},{8,24},{16,0},{24,8},{1,17},{9,25},{17,1},{25,9},{2,18},{10... | collective-permute-start | bytes 663560 | tf_op jit(solution)/shard_map/ppermute | solution.py:658
  186.8 10.8 %collective-permute-start.15 = (bf16[144,768]{1,0:T(8,128)(2,1)}, bf16[144,768]{1,0:T(8,128)(2,1)}, u32[]{:S(2)}, u32[]{:S(2)}) collective-permute-start(bf16[144,768]{1,0:T(8,128)(2,1)} %get-tuple-element.77), channel_id=1, source_target_pairs={{0,24},{8,16},{16,8},{24,0},{1,25},{9,17},{17,9},{25,1},{2,26},{10... | collective-permute-start | bytes 663560 | tf_op jit(solution)/shard_map/ppermute | solution.py:658
  197.6 42.4 %all-to-all-start.1 = ((bf16[8,256,768]{2,1,0:T(8,128)(2,1)}), bf16[8,256,768]{2,1,0:T(8,128)(2,1)}, u32[]{:S(2)}, u32[]{:S(2)}) async-start(bf16[8,256,768]{2,1,0:T(8,128)(2,1)} %get-tuple-element.79), calls=%async_computation.1 | async-start | bytes 6291456 | tf_op jit(solution)/shard_map/all_to_all | solution.py:717
  203.3 1.5 collective-permute-start.16
  204.9 7.8 %collective-permute-start.17 = (bf16[144,768]{1,0:T(8,128)(2,1)S(1)}, bf16[144,768]{1,0:T(8,128)(2,1)S(1)}, u32[]{:S(2)}, u32[]{:S(2)}) collective-permute-start(bf16[144,768]{1,0:T(8,128)(2,1)S(1)} %add_convert_fusion.2), channel_id=1, source_target_pairs={{0,2},{2,0},{4,6},{6,4},{1,3},{3,1},{5,7},{7,5},{8,10},{10,8},{12,... | collective-permute-start | bytes 663560 | tf_op jit(solution)/shard_map/ppermute | solution.py:735
  212.8 12.7 %collective-permute-start.18 = (bf16[144,768]{1,0:T(8,128)(2,1)S(1)}, bf16[144,768]{1,0:T(8,128)(2,1)S(1)}, u32[]{:S(2)}, u32[]{:S(2)}) collective-permute-start(bf16[144,768]{1,0:T(8,128)(2,1)S(1)} %add_convert_fusion.1), channel_id=1, source_target_pairs={{0,4},{2,6},{4,0},{6,2},{1,5},{3,7},{5,1},{7,3},{8,12},{10,14},{12... | collective-permute-start | bytes 663560 | tf_op jit(solution)/shard_map/ppermute | solution.py:735

commit v3 on v2

--- a/solution.py
+++ b/solution.py
@@ -297,7 +297,7 @@
             qkv_ref[:, cols] = (dot(x_ref[...], slab[:, cols]) * scale).astype(BF)
         return carry
 
-    lax.fori_loop(0, 3, part, 0)
+    lax.fori_loop(0, 3, part, 0, unroll=True)
 
 
 def attend(qkv_ref, bias_v, p_v, c_ref):
@@ -354,7 +354,7 @@
         dqkv[:, cols(2)] = jnp.concatenate(dv, axis=0).T.astype(BF)
         return carry
 
-    lax.fori_loop(0, HEADS // 2, body, 0, unroll=6)
+    lax.fori_loop(0, HEADS // 2, body, 0, unroll=3)
 
 
 def by_columns(target, value, step=256):

time: 244 us -> 244 us (level)
  transfers between devices with their start and end apart: 21 -> 21, of which waited for: 12 -> 12; matrix products, arithmetic and copies ran while one was open for 7% -> 7% of each run, Pallas kernels for 19% -> 18%
where the time goes in v3:
time: 244 us; the launch traced here: 243 us
  waiting for transfers between devices  95.8 us (39%)
  Pallas kernels  93.7 us (38%)
  starting transfers between devices  30 us (12%)
  other arithmetic  11.1 us (5%)
  local copies, waits for them, and re-layouts  11.1 us (5%)
    pallas_call x4, Pallas kernels, run(): pl.pallas_call(wrapped, out_shape=[shape for shape, _ in outs], in_specs=...  93.7 us
    ppermute x6, waiting for transfers between devices, sect(): return lax.ppermute(x, 'section', [(i, i ^ apart) for i in sections])  37.4 us
    ppermute x3, waiting for transfers between devices, by_core(): return lax.ppermute(x, ('section', 'core'), pairs)  26.4 us
    ppermute x2, waiting for transfers between devices, per_device(): lax.ppermute(total, 'group', [(i, i ^ apart) for i in range(n_group)])  13.4 us
    all_to_all x2, waiting for transfers between devices, to_owners(): return lax.all_to_all(x, ('section', 'core'), 0, 0, tiled=True)  12.6 us
    all_to_all x2, starting transfers between devices, to_owners(): return lax.all_to_all(x, ('section', 'core'), 0, 0, tiled=True)  8.72 us
    ppermute x6, starting transfers between devices, sect(): return lax.ppermute(x, 'section', [(i, i ^ apart) for i in sections])  7.18 us
    ppermute x3, starting transfers between devices, by_core(): return lax.ppermute(x, ('section', 'core'), pairs)  6.78 us
  transfers between devices with their start and end apart: 21, of which 12 were waited for; matrix products, arithmetic and copies ran while one was open for 7% of the time, Pallas kernels for 18%

profile of v3, /device:TPU:0, one launch (start us, length us, event | category | flops | bytes accessed | tf_op | source)
XLA Modules:
  0.0 242.8 jit_solution(14353112739926983218)
XLA Ops:
  0.6 0.9 convert.10
  1.6 0.9 convert_bitcast_fusion
  2.6 0.0 copy-start.2
  2.6 1.9 dynamic-slice_bitcast_fusion
  4.5 1.6 pad_maximum_fusion
  6.1 3.0 %collective-permute-start = (bf16[400,3072]{1,0:T(8,128)(2,1)}, bf16[400,3072]{1,0:T(8,128)(2,1)S(1)}, u32[]{:S(2)}, u32[]{:S(2)}) collective-permute-start(bf16[400,3072]{1,0:T(8,128)(2,1)} %pad_maximum_fusion), channel_id=1, source_target_pairs={{0,16},{1,9},{8,24},{9,1},{16,0},{17,25},{24,8},{25,17},{2,18},{3,... | collective-permute-start | bytes 7372808 | tf_op jit(solution)/shard_map/ppermute | solution.py:665
  9.1 1.3 dynamic-slice_bitcast_fusion.1
  10.4 0.0 copy-start.8
  10.4 0.0 copy-start.5
  10.4 0.0 copy-start.6
  10.5 0.0 copy-start.7
  10.5 1.1 pad_maximum_fusion.1
  11.6 1.5 collective-permute-start.1
  13.1 2.0 dynamic-slice_bitcast_fusion.5
  15.1 1.9 dynamic-slice_bitcast_fusion.3
  17.0 0.5 collective-permute-start.3
  17.6 0.6 collective-permute-start.4
  18.2 0.1 collective-permute-start.5
  18.2 1.9 pad_maximum_fusion.2.refs_1_
  20.2 2.9 %collective-permute-start.6 = (f32[8,768]{1,0:T(8,128)S(1)}, f32[8,768]{1,0:T(8,128)S(1)}, u32[]{:S(2)}, u32[]{:S(2)}) collective-permute-start(f32[8,768]{1,0:T(8,128)S(1)} %concatenate.28), channel_id=1, source_target_pairs={{0,24},{8,16},{16,8},{24,0},{1,25},{9,17},{17,9},{25,1},{2,26},{10... | collective-permute-start | bytes 73736 | tf_op jit(solution)/shard_map/ppermute | solution.py:658
  23.1 1.9 pad_maximum_fusion.3.refs_1_
  25.0 18.4 %collective-permute-done.4 = f32[8,768]{1,0:T(8,128)S(1)} collective-permute-done((f32[8,768]{1,0:T(8,128)S(1)}, f32[8,768]{1,0:T(8,128)S(1)}, u32[]{:S(2)}, u32[]{:S(2)}) %collective-permute-start.4) | collective-permute-done | bytes 24608 | tf_op jit(solution)/shard_map/ppermute | solution.py:658
  43.4 8.3 %collective-permute-done.5 = f32[8,768]{1,0:T(8,128)S(1)} collective-permute-done((f32[8,768]{1,0:T(8,128)S(1)}, f32[8,768]{1,0:T(8,128)S(1)}, u32[]{:S(2)}, u32[]{:S(2)}) %collective-permute-start.5) | collective-permute-done | bytes 24608 | tf_op jit(solution)/shard_map/ppermute | solution.py:658
  51.7 0.0 copy-start.1
  51.7 2.3 collective-permute-start.8
  54.0 1.6 collective-permute-start.7
  55.6 26.4 %collective-permute-done.8.refs_11_.refs_9_ = bf16[400,3072]{1,0:T(8,128)(2,1)} collective-permute-done((bf16[400,3072]{1,0:T(8,128)(2,1)S(1)}, bf16[400,3072]{1,0:T(8,128)(2,1)}, u32[]{:S(2)}, u32[]{:S(2)}) %collective-permute-start.8) | collective-permute-done | bytes 2457632 | tf_op jit(solution)/shard_map/ppermute | solution.py:665
  82.0 0.5 collective-permute-start.9
  82.5 0.3 collective-permute-done.7.refs_9_.refs_7_
  82.8 0.8 fusion.3
  83.6 0.9 copy.19.refs_2_
  84.5 0.1 stack.110
  84.6 0.1 stack.105
  84.6 0.1 stack.100
  84.7 0.1 stack.95
  84.8 0.6 pad_add_fusion.refs_0_
  85.4 0.6 pad_maximum_fusion.5.refs_4_.refs_2_
  86.1 2.8 %collective-permute-done.9.refs_12_.refs_10_ = bf16[208,3072]{1,0:T(8,128)(2,1)} collective-permute-done((bf16[208,3072]{1,0:T(8,128)(2,1)}, bf16[208,3072]{1,0:T(8,128)(2,1)}, u32[]{:S(2)}, u32[]{:S(2)}) %collective-permute-start.9) | collective-permute-done | bytes 1277984 | tf_op jit(solution)/shard_map/ppermute | solution.py:661
  88.8 1.8 collective-permute-done.10.refs_13_.refs_11_
  90.7 46.8 %forward.1 = (bf16[2,512,2304]{2,1,0:T(8,128)(2,1)}, bf16[2,512,768]{2,1,0:T(8,128)(2,1)}, bf16[2,12,512,512]{3,2,1,0:T(8,128)(2,1)}, bf16[2,512,768]{2,1,0:T(8,...) custom-call(s32[4,5]{1,0:T(4,128)} %pad_add_fusion.refs_0_, ...), custom_call_target="tpu_custom_call" | custom-call | flops 6000000000 | tf_op jit(solution)/shard_map/forward/pallas_call | solution.py:52
  137.4 4.3 %all-to-all-start = ((bf16[8,256,768]{2,1,0:T(8,128)(2,1)}), bf16[8,256,768]{2,1,0:T(8,128)(2,1)S(1)}, u32[]{:S(2)}, u32[]{:S(2)}) async-start(bf16[8,256,768]{2,1,0:T(8,128)(2,1)} %get-tuple-element.53), calls=%async_computation | async-start | bytes 6291456 | tf_op jit(solution)/shard_map/all_to_all | solution.py:717
  141.7 41.5 %backward.1 = (bf16[8,256,768]{2,1,0:T(8,128)(2,1)}, bf16[144,768]{1,0:T(8,128)(2,1)}, bf16[144,768]{1,0:T(8,128)(2,1)}, bf16[144,768]{1,0:T(8,128)(2,1)}, bf16[144,768]{1,0:T(8,128)(2,1)}) custom-call(s32[4,5]{1,0:T(4,128)} %pad_add_fusion.refs_0_, bf16[512,768]{1,0:T(8,128)(2,1)} %pad_maximum_fusion.3.refs_1_, ...), custom_call_target="tpu_custom_call" | custom-call | flops 6000000000 | tf_op jit(solution)/shard_map/backward/pallas_call | solution.py:52
  183.2 0.0 copy-start
  183.2 2.1 collective-permute-start.13
  185.3 1.5 collective-permute-start.14
  186.8 0.1 collective-permute-start.15
  186.9 5.0 %collective-permute-done.13 = bf16[144,768]{1,0:T(8,128)(2,1)} collective-permute-done((bf16[144,768]{1,0:T(8,128)(2,1)}, bf16[144,768]{1,0:T(8,128)(2,1)}, u32[]{:S(2)}, u32[]{:S(2)}) %collective-permute-start.13) | collective-permute-done | bytes 221216 | tf_op jit(solution)/shard_map/ppermute | solution.py:658
  191.8 5.7 %collective-permute-done.14 = bf16[144,768]{1,0:T(8,128)(2,1)} collective-permute-done((bf16[144,768]{1,0:T(8,128)(2,1)}, bf16[144,768]{1,0:T(8,128)(2,1)}, u32[]{:S(2)}, u32[]{:S(2)}) %collective-permute-start.14) | collective-permute-done | bytes 221216 | tf_op jit(solution)/shard_map/ppermute | solution.py:658
  197.6 4.5 %all-to-all-start.1 = ((bf16[8,256,768]{2,1,0:T(8,128)(2,1)}), bf16[8,256,768]{2,1,0:T(8,128)(2,1)}, u32[]{:S(2)}, u32[]{:S(2)}) async-start(bf16[8,256,768]{2,1,0:T(8,128)(2,1)} %get-tuple-element.79), calls=%async_computation.1 | async-start | bytes 6291456 | tf_op jit(solution)/shard_map/all_to_all | solution.py:717
  202.1 1.3 add_convert_fusion.3
  203.3 0.4 collective-permute-start.16
  203.8 1.1 collective-permute-done.16
  204.9 0.1 add_convert_fusion.2
  204.9 1.7 collective-permute-start.17
  206.6 6.1 %collective-permute-done.17 = bf16[144,768]{1,0:T(8,128)(2,1)S(1)} collective-permute-done((bf16[144,768]{1,0:T(8,128)(2,1)S(1)}, bf16[144,768]{1,0:T(8,128)(2,1)S(1)}, u32[]{:S(2)}, u32[]{:S(2)}) %collective-permute-start.17) | collective-permute-done | bytes 221216 | tf_op jit(solution)/shard_map/ppermute | solution.py:735
  212.7 0.1 add_convert_fusion.1
  212.8 2.7 %collective-permute-start.18 = (bf16[144,768]{1,0:T(8,128)(2,1)S(1)}, bf16[144,768]{1,0:T(8,128)(2,1)S(1)}, u32[]{:S(2)}, u32[]{:S(2)}) collective-permute-start(bf16[144,768]{1,0:T(8,128)(2,1)S(1)} %add_convert_fusion.1), channel_id=1, source_target_pairs={{0,4},{2,6},{4,0},{6,2},{1,5},{3,7},{5,1},{7,3},{8,12},{10,14},{12... | collective-permute-start | bytes 663560 | tf_op jit(solution)/shard_map/ppermute | solution.py:735
  215.4 2.7 %settle.2 = bf16[8,256,768]{2,1,0:T(8,128)(2,1)} custom-call(bf16[8,256,768]{2,1,0:T(8,128)(2,1)} %copy-done), custom_call_target="tpu_custom_call" | custom-call | flops 300000000 | tf_op jit(solution)/shard_map/settle/pallas_call | solution.py:52
  218.1 7.3 %collective-permute-done.18 = bf16[144,768]{1,0:T(8,128)(2,1)S(1)} collective-permute-done((bf16[144,768]{1,0:T(8,128)(2,1)S(1)}, bf16[144,768]{1,0:T(8,128)(2,1)S(1)}, u32[]{:S(2)}, u32[]{:S(2)}) %collective-permute-start.18) | collective-permute-done | bytes 221216 | tf_op jit(solution)/shard_map/ppermute | solution.py:735
  225.5 0.5 slice.57
  226.0 0.6 fusion.1
  226.6 0.8 slice_bitcast_fusion
  227.4 12.6 %all-to-all-done.1.refs_0_ = bf16[8,256,768]{2,1,0:T(8,128)(2,1)} async-done(((bf16[8,256,768]{2,1,0:T(8,128)(2,1)}), bf16[8,256,768]{2,1,0:T(8,128)(2,1)}, u32[]{:S(2)}, u32[]{:S(2)}) %all-to-all-start.1) | async-done | bytes 3145760 | tf_op jit(solution)/shard_map/all_to_all | solution.py:717
  240.0 2.7 %settle.3 = bf16[8,256,768]{2,1,0:T(8,128)(2,1)} custom-call(bf16[8,256,768]{2,1,0:T(8,128)(2,1)} %all-to-all-done.1.refs_0_), custom_call_target="tpu_custom_call" | custom-call | flops 300000000 | tf_op jit(solution)/shard_map/settle/pallas_call | solution.py:52
  (33 shorter events, 0.2 us)
Async XLA Ops:
  2.6 1.9 copy-start.2
  6.1 45.5 %collective-permute-start = (bf16[400,3072]{1,0:T(8,128)(2,1)}, bf16[400,3072]{1,0:T(8,128)(2,1)S(1)}, u32[]{:S(2)}, u32[]{:S(2)}) collective-permute-start(bf16[400,3072]{1,0:T(8,128)(2,1)} %pad_maximum_fusion), channel_id=1, source_target_pairs={{0,16},{1,9},{8,24},{9,1},{16,0},{17,25},{24,8},{25,17},{2,18},{3,... | collective-permute-start | bytes 7372808 | tf_op jit(solution)/shard_map/ppermute | solution.py:665
  10.4 7.1 %copy-start.8 = (f32[1,64]{1,0:T(1,128)S(1)}, f32[1,64]{1,0:T(1,128)}, u32[]{:S(2)}) copy-start(f32[1,64]{1,0:T(1,128)} %param.17) | copy-start | bytes 772
  10.4 7.1 %copy-start.5 = (f32[1,768]{1,0:T(1,128)S(1)}, f32[1,768]{1,0:T(1,128)}, u32[]{:S(2)}) copy-start(f32[1,768]{1,0:T(1,128)} %param.19) | copy-start | bytes 9220
  10.4 7.1 %copy-start.6 = (f32[1,768]{1,0:T(1,128)S(1)}, f32[1,768]{1,0:T(1,128)}, u32[]{:S(2)}) copy-start(f32[1,768]{1,0:T(1,128)} %param.20) | copy-start | bytes 9220
  10.5 7.1 %copy-start.7 = (f32[1,768]{1,0:T(1,128)S(1)}, f32[1,768]{1,0:T(1,128)}, u32[]{:S(2)}) copy-start(f32[1,768]{1,0:T(1,128)} %param.21) | copy-start | bytes 9220
  11.6 40.0 %collective-permute-start.1 = (bf16[208,3072]{1,0:T(8,128)(2,1)}, bf16[208,3072]{1,0:T(8,128)(2,1)}, u32[]{:S(2)}, u32[]{:S(2)}) collective-permute-start(bf16[208,3072]{1,0:T(8,128)(2,1)} %pad_maximum_fusion.1), channel_id=1, source_target_pairs={{0,8},{1,17},{8,0},{9,25},{16,24},{17,1},{24,16},{25,9},{2,10},{3,... | collective-permute-start | bytes 3833864 | tf_op jit(solution)/shard_map/ppermute | solution.py:665
  15.1 3.1 %collective-permute-start.2 = (bf16[256,768]{1,0:T(8,128)(2,1)}, bf16[256,768]{1,0:T(8,128)(2,1)}, u32[]{:S(2)}, u32[]{:S(2)}) collective-permute-start(bf16[256,768]{1,0:T(8,128)(2,1)} %get-tuple-element.87), channel_id=1, source_target_pairs={{0,1},{1,0},{2,3},{3,2},{4,5},{5,4},{6,7},{7,6},{8,9},{9,8},{10,11... | collective-permute-start | bytes 1179656 | tf_op jit(solution)/shard_map/ppermute | solution.py:661
  17.0 3.2 %collective-permute-start.3 = (bf16[256,768]{1,0:T(8,128)(2,1)}, bf16[256,768]{1,0:T(8,128)(2,1)}, u32[]{:S(2)}, u32[]{:S(2)}) collective-permute-start(bf16[256,768]{1,0:T(8,128)(2,1)} %get-tuple-element.85), channel_id=1, source_target_pairs={{0,1},{1,0},{2,3},{3,2},{4,5},{5,4},{6,7},{7,6},{8,9},{9,8},{10,11... | collective-permute-start | bytes 1179656 | tf_op jit(solution)/shard_map/ppermute | solution.py:661
  17.6 25.8 %collective-permute-start.4 = (f32[8,768]{1,0:T(8,128)S(1)}, f32[8,768]{1,0:T(8,128)S(1)}, u32[]{:S(2)}, u32[]{:S(2)}) collective-permute-start(f32[8,768]{1,0:T(8,128)S(1)} %concatenate.28), channel_id=1, source_target_pairs={{0,8},{8,0},{16,24},{24,16},{1,9},{9,1},{17,25},{25,17},{2,10},{10... | collective-permute-start | bytes 73736 | tf_op jit(solution)/shard_map/ppermute | solution.py:658
  18.2 33.5 %collective-permute-start.5 = (f32[8,768]{1,0:T(8,128)S(1)}, f32[8,768]{1,0:T(8,128)S(1)}, u32[]{:S(2)}, u32[]{:S(2)}) collective-permute-start(f32[8,768]{1,0:T(8,128)S(1)} %concatenate.28), channel_id=1, source_target_pairs={{0,16},{8,24},{16,0},{24,8},{1,17},{9,25},{17,1},{25,9},{2,18},{10... | collective-permute-start | bytes 73736 | tf_op jit(solution)/shard_map/ppermute | solution.py:658
  20.2 31.5 %collective-permute-start.6 = (f32[8,768]{1,0:T(8,128)S(1)}, f32[8,768]{1,0:T(8,128)S(1)}, u32[]{:S(2)}, u32[]{:S(2)}) collective-permute-start(f32[8,768]{1,0:T(8,128)S(1)} %concatenate.28), channel_id=1, source_target_pairs={{0,24},{8,16},{16,8},{24,0},{1,25},{9,17},{17,9},{25,1},{2,26},{10... | collective-permute-start | bytes 73736 | tf_op jit(solution)/shard_map/ppermute | solution.py:658
  51.7 39.0 %copy-start.1 = (bf16[400,3072]{1,0:T(8,128)(2,1)}, bf16[400,3072]{1,0:T(8,128)(2,1)S(1)}, u32[]{:S(2)}) copy-start(bf16[400,3072]{1,0:T(8,128)(2,1)S(1)} %collective-permute-done.refs_10_.refs_8_) | copy-start | bytes 7372804
  51.7 30.3 %collective-permute-start.8 = (bf16[400,3072]{1,0:T(8,128)(2,1)S(1)}, bf16[400,3072]{1,0:T(8,128)(2,1)}, u32[]{:S(2)}, u32[]{:S(2)}) collective-permute-start(bf16[400,3072]{1,0:T(8,128)(2,1)S(1)} %collective-permute-done.refs_10_.refs_8_), channel_id=1, source_target_pairs={{0,8},{1,17},{8,0},{9,25},{16,24},{17,1},{24,16},{25,9},{2,10},{3,... | collective-permute-start | bytes 7372808 | tf_op jit(solution)/shard_map/ppermute | solution.py:665
  54.0 28.8 %collective-permute-start.7 = (bf16[208,3072]{1,0:T(8,128)(2,1)}, bf16[208,3072]{1,0:T(8,128)(2,1)}, u32[]{:S(2)}, u32[]{:S(2)}) collective-permute-start(bf16[208,3072]{1,0:T(8,128)(2,1)} %collective-permute-done.1.refs_8_.refs_6_), channel_id=1, source_target_pairs={{0,2},{2,0},{4,6},{6,4},{1,3},{3,1},{5,7},{7,5},{8,10},{10,8},{12,... | collective-permute-start | bytes 3833864 | tf_op jit(solution)/shard_map/ppermute | solution.py:694
  55.6 33.3 %collective-permute-start.11 = (bf16[400,3072]{1,0:T(8,128)(2,1)S(1)}, bf16[400,3072]{1,0:T(8,128)(2,1)}, u32[]{:S(2)}, u32[]{:S(2)}) collective-permute-start(bf16[400,3072]{1,0:T(8,128)(2,1)S(1)} %collective-permute-done.refs_10_.refs_8_), channel_id=1, source_target_pairs={{0,1},{1,0},{2,3},{3,2},{4,5},{5,4},{6,7},{7,6},{8,9},{9,8},{10,11... | collective-permute-start | bytes 7372808 | tf_op jit(solution)/shard_map/ppermute | solution.py:661
  82.0 8.7 %collective-permute-start.12 = (bf16[400,3072]{1,0:T(8,128)(2,1)}, bf16[400,3072]{1,0:T(8,128)(2,1)}, u32[]{:S(2)}, u32[]{:S(2)}) collective-permute-start(bf16[400,3072]{1,0:T(8,128)(2,1)} %collective-permute-done.8.refs_11_.refs_9_), channel_id=1, source_target_pairs={{0,1},{1,0},{2,3},{3,2},{4,5},{5,4},{6,7},{7,6},{8,9},{9,8},{10,11... | collective-permute-start | bytes 7372808 | tf_op jit(solution)/shard_map/ppermute | solution.py:661
  82.0 6.8 %collective-permute-start.9 = (bf16[208,3072]{1,0:T(8,128)(2,1)}, bf16[208,3072]{1,0:T(8,128)(2,1)}, u32[]{:S(2)}, u32[]{:S(2)}) collective-permute-start(bf16[208,3072]{1,0:T(8,128)(2,1)} %collective-permute-done.1.refs_8_.refs_6_), channel_id=1, source_target_pairs={{0,1},{1,0},{2,3},{3,2},{4,5},{5,4},{6,7},{7,6},{8,9},{9,8},{10,11... | collective-permute-start | bytes 3833864 | tf_op jit(solution)/shard_map/ppermute | solution.py:661
  82.8 7.9 %collective-permute-start.10 = (bf16[208,3072]{1,0:T(8,128)(2,1)}, bf16[208,3072]{1,0:T(8,128)(2,1)}, u32[]{:S(2)}, u32[]{:S(2)}) collective-permute-start(bf16[208,3072]{1,0:T(8,128)(2,1)} %collective-permute-done.7.refs_9_.refs_7_), channel_id=1, source_target_pairs={{0,1},{1,0},{2,3},{3,2},{4,5},{5,4},{6,7},{7,6},{8,9},{9,8},{10,11... | collective-permute-start | bytes 3833864 | tf_op jit(solution)/shard_map/ppermute | solution.py:661
  83.6 7.1 %copy-start.4 = (s32[512]{0:T(512)}, s32[512]{0:T(512)S(1)}, u32[]{:S(2)}) copy-start(s32[512]{0:T(512)S(1)} %pad_add_fusion.1) | copy-start | bytes 6148
  137.4 45.8 %all-to-all-start = ((bf16[8,256,768]{2,1,0:T(8,128)(2,1)}), bf16[8,256,768]{2,1,0:T(8,128)(2,1)S(1)}, u32[]{:S(2)}, u32[]{:S(2)}) async-start(bf16[8,256,768]{2,1,0:T(8,128)(2,1)} %get-tuple-element.53), calls=%async_computation | async-start | bytes 6291456 | tf_op jit(solution)/shard_map/all_to_all | solution.py:717
  183.2 14.4 %copy-start = (bf16[8,256,768]{2,1,0:T(8,128)(2,1)}, bf16[8,256,768]{2,1,0:T(8,128)(2,1)S(1)}, u32[]{:S(2)}) copy-start(bf16[8,256,768]{2,1,0:T(8,128)(2,1)S(1)} %all-to-all-done.refs_0_) | copy-start | bytes 9437188
  183.2 18.8 %copy-start.3 = (bf16[144,768]{1,0:T(8,128)(2,1)S(1)}, bf16[144,768]{1,0:T(8,128)(2,1)}, u32[]{:S(2)}) copy-start(bf16[144,768]{1,0:T(8,128)(2,1)} %get-tuple-element.80) | copy-start | bytes 663556
  183.2 8.6 %collective-permute-start.13 = (bf16[144,768]{1,0:T(8,128)(2,1)}, bf16[144,768]{1,0:T(8,128)(2,1)}, u32[]{:S(2)}, u32[]{:S(2)}) collective-permute-start(bf16[144,768]{1,0:T(8,128)(2,1)} %get-tuple-element.75), channel_id=1, source_target_pairs={{0,8},{8,0},{16,24},{24,16},{1,9},{9,1},{17,25},{25,17},{2,10},{10... | collective-permute-start | bytes 663560 | tf_op jit(solution)/shard_map/ppermute | solution.py:658
  185.3 12.3 %collective-permute-start.14 = (bf16[144,768]{1,0:T(8,128)(2,1)}, bf16[144,768]{1,0:T(8,128)(2,1)}, u32[]{:S(2)}, u32[]{:S(2)}) collective-permute-start(bf16[144,768]{1,0:T(8,128)(2,1)} %get-tuple-element.76), channel_id=1, source_target_pairs={{0,16},{8,24},{16,0},{24,8},{1,17},{9,25},{17,1},{25,9},{2,18},{10... | collective-permute-start | bytes 663560 | tf_op jit(solution)/shard_map/ppermute | solution.py:658
  186.8 10.8 %collective-permute-start.15 = (bf16[144,768]{1,0:T(8,128)(2,1)}, bf16[144,768]{1,0:T(8,128)(2,1)}, u32[]{:S(2)}, u32[]{:S(2)}) collective-permute-start(bf16[144,768]{1,0:T(8,128)(2,1)} %get-tuple-element.77), channel_id=1, source_target_pairs={{0,24},{8,16},{16,8},{24,0},{1,25},{9,17},{17,9},{25,1},{2,26},{10... | collective-permute-start | bytes 663560 | tf_op jit(solution)/shard_map/ppermute | solution.py:658
  197.6 42.4 %all-to-all-start.1 = ((bf16[8,256,768]{2,1,0:T(8,128)(2,1)}), bf16[8,256,768]{2,1,0:T(8,128)(2,1)}, u32[]{:S(2)}, u32[]{:S(2)}) async-start(bf16[8,256,768]{2,1,0:T(8,128)(2,1)} %get-tuple-element.79), calls=%async_computation.1 | async-start | bytes 6291456 | tf_op jit(solution)/shard_map/all_to_all | solution.py:717
  203.3 1.5 collective-permute-start.16
  204.9 7.8 %collective-permute-start.17 = (bf16[144,768]{1,0:T(8,128)(2,1)S(1)}, bf16[144,768]{1,0:T(8,128)(2,1)S(1)}, u32[]{:S(2)}, u32[]{:S(2)}) collective-permute-start(bf16[144,768]{1,0:T(8,128)(2,1)S(1)} %add_convert_fusion.2), channel_id=1, source_target_pairs={{0,2},{2,0},{4,6},{6,4},{1,3},{3,1},{5,7},{7,5},{8,10},{10,8},{12,... | collective-permute-start | bytes 663560 | tf_op jit(solution)/shard_map/ppermute | solution.py:735
  212.8 12.7 %collective-permute-start.18 = (bf16[144,768]{1,0:T(8,128)(2,1)S(1)}, bf16[144,768]{1,0:T(8,128)(2,1)S(1)}, u32[]{:S(2)}, u32[]{:S(2)}) collective-permute-start(bf16[144,768]{1,0:T(8,128)(2,1)S(1)} %add_convert_fusion.1), channel_id=1, source_target_pairs={{0,4},{2,6},{4,0},{6,2},{1,5},{3,7},{5,1},{7,3},{8,12},{10,14},{12... | collective-permute-start | bytes 663560 | tf_op jit(solution)/shard_map/ppermute | solution.py:735
